TPU v7x, 32 devices: a whole 2x2x4 slice. The times are simulated.
32 devices in a mesh: groups: 2 (over y), ctx: 16 (over z, x, core).
Axes of the slice: x: 2, y: 2, z: 4, core: 2. Of those that a mesh axis runs over, the one named last changes fastest.
Arguments:
- query_rows: bfloat16 [4096, 2560], P(('groups', 'ctx')), parts along dimension 0, may hold values from -211 to 211
- key_rows: bfloat16 [4096, 2560], P(('groups', 'ctx')), parts along dimension 0, may hold values from -6.2 to 6.2
- value_rows: bfloat16 [4096, 2560], P(('groups', 'ctx')), parts along dimension 0, may hold values from -6 to 6
- out_grad: bfloat16 [4096, 2560], P(('groups', 'ctx')), parts along dimension 0, may hold values from -6 to 6
- selected: int32 [32, 8], P('groups'), parts along dimension 0, may hold values from 0 to 15, as said below
Outputs:
- attended: bfloat16 [4096, 2560], P(('groups', 'ctx')), parts along dimension 0
- grad_query: bfloat16 [4096, 2560], P(('groups', 'ctx')), parts along dimension 0
- grad_key: bfloat16 [4096, 2560], P(('groups', 'ctx')), parts along dimension 0
- grad_value: bfloat16 [4096, 2560], P(('groups', 'ctx')), parts along dimension 0
- pooled_key_grad: float32 [64, 2560], P(('groups', 'ctx')), parts along dimension 0
- pooled_value_grad: float32 [64, 2560], P(('groups', 'ctx')), parts along dimension 0
There are 2 independent parts, one for each index of `groups`. A program takes and returns all parts, laid end to end along the dimension named above; each array names one. Nothing has to cross between parts.
Inputs may be any that keep to these rules, and one draw needn't show every extreme that they name: `selected`: each row names 8 different tiles.
All inputs are finite; a program needn't handle non-finite values.
Results may differ from a plain program's by a relative error of at most 0.029.
Values may be sent and summed in bfloat16 or wider, within the bound.
No kernel may reach another device: no remote copies, remote signals or barrier semaphores. Data moves between devices by JAX's collectives and lax.ppermute only.
A program may use at most 192 MiB of HBM per device.

v0:
```python
import jax
import jax.numpy as jnp
from jax import lax
from jax.sharding import PartitionSpec as P

HEADS = 20
HEAD_DIM = 128
TILE = 128
POOL = 64
SEL = 8


def pooled(rows):
    return jnp.mean(rows.astype(jnp.float32).reshape(-1, POOL, rows.shape[1]), axis=1).astype(
        jnp.bfloat16
    )


def contract(left, right, left_dim, right_dim):
    return lax.dot_general(
        left, right, (((left_dim,), (right_dim,)), ((), ())), preferred_element_type=jnp.float32
    )


def attend(queries, grads_out, keys_all, values_all):
    scaling = HEAD_DIM ** (-0.5)
    out_parts, query_parts, key_parts, value_parts = ([], [], [], [])
    for head in range(HEADS):
        lower = head * HEAD_DIM
        upper = lower + HEAD_DIM
        head_query = queries[:, lower:upper]
        head_grad = grads_out[:, lower:upper]
        head_key = keys_all[:, lower:upper]
        head_value = values_all[:, lower:upper]
        scores = contract(head_query, head_key, 1, 1) * scaling
        summit = jnp.max(scores, axis=-1, keepdims=True)
        raised = jnp.exp(scores - summit)
        weights = raised / jnp.sum(raised, axis=-1, keepdims=True)
        rounded = weights.astype(jnp.bfloat16)
        out_rows = jnp.dot(rounded, head_value, preferred_element_type=jnp.float32).astype(
            jnp.bfloat16
        )
        row_dots = jnp.sum(
            head_grad.astype(jnp.float32) * out_rows.astype(jnp.float32), axis=-1, keepdims=True
        )
        prob_grad = contract(head_grad, head_value, 1, 1)
        score_grad = (weights * (prob_grad - row_dots)).astype(jnp.bfloat16)
        query_grad = jnp.dot(score_grad, head_key, preferred_element_type=jnp.float32) * scaling
        key_terms = contract(score_grad, head_query, 0, 0) * scaling
        value_terms = contract(rounded, head_grad, 0, 0)
        out_parts.append(out_rows)
        query_parts.append(query_grad.astype(jnp.bfloat16))
        key_parts.append(key_terms)
        value_parts.append(value_terms)
    return (
        jnp.concatenate(out_parts, axis=1),
        jnp.concatenate(query_parts, axis=1),
        jnp.concatenate(key_parts, axis=1),
        jnp.concatenate(value_parts, axis=1),
    )


def package(tiles_in, pooled_in, devices, spread):
    tiles_here, tile_len, columns = tiles_in.shape
    per_tile = tile_len // POOL
    split_rows = tiles_in.reshape(tiles_here, devices, spread, columns)
    copies = jnp.broadcast_to(
        pooled_in.reshape(tiles_here, 1, per_tile, columns),
        (tiles_here, devices, per_tile, columns),
    )
    return jnp.concatenate([split_rows, copies], axis=2).reshape(
        tiles_here, devices * (spread + per_tile), columns
    )


def shards(query_rows, key_rows, value_rows, out_grad, selected):
    height, columns = query_rows.shape
    devices = lax.axis_size("ctx")
    tiles_here = height // TILE
    spread = TILE // devices
    own_keys = pooled(key_rows)
    own_values = pooled(value_rows)
    key_tiles = key_rows.reshape(tiles_here, TILE, columns)
    value_tiles = value_rows.reshape(tiles_here, TILE, columns)
    joined_keys, joined_values = (
        lax.all_to_all(
            package(key_tiles, own_keys, devices, spread),
            "ctx",
            split_axis=1,
            concat_axis=0,
            tiled=True,
        ),
        lax.all_to_all(
            package(value_tiles, own_values, devices, spread),
            "ctx",
            split_axis=1,
            concat_axis=0,
            tiled=True,
        ),
    )
    held_keys = joined_keys[:, :spread]
    held_values = joined_values[:, :spread]
    pool_keys = joined_keys[:, spread:].reshape(-1, columns)
    pool_values = joined_values[:, spread:].reshape(-1, columns)
    comp_count = pool_keys.shape[0]
    got_keys, got_values = (
        lax.all_to_all(held_keys[selected], "ctx", split_axis=0, concat_axis=2, tiled=True),
        lax.all_to_all(held_values[selected], "ctx", split_axis=0, concat_axis=2, tiled=True),
    )
    fine_keys = got_keys.reshape(tiles_here, SEL * TILE, columns)
    fine_values = got_values.reshape(tiles_here, SEL * TILE, columns)
    out_tiles, query_tiles, key_listed, value_listed = ([], [], [], [])
    keys_all = jnp.concatenate([pool_keys, fine_keys[0]], axis=0)
    values_all = jnp.concatenate([pool_values, fine_values[0]], axis=0)
    out_rows, query_grad, key_terms, value_terms = attend(
        query_rows, out_grad, keys_all, values_all
    )
    out_tiles.append(out_rows)
    query_tiles.append(query_grad)
    coarse_keys = key_terms[:comp_count]
    coarse_values = value_terms[:comp_count]
    key_listed.append(key_terms[comp_count:].astype(jnp.bfloat16))
    value_listed.append(value_terms[comp_count:].astype(jnp.bfloat16))
    own_coarse_keys, own_coarse_values = (
        lax.psum_scatter(coarse_keys, "ctx", scatter_dimension=0, tiled=True),
        lax.psum_scatter(coarse_values, "ctx", scatter_dimension=0, tiled=True),
    )
    listed_keys = jnp.stack(key_listed).reshape(tiles_here * SEL, devices, spread, columns)
    listed_values = jnp.stack(value_listed).reshape(tiles_here * SEL, devices, spread, columns)
    back_keys, back_values = (
        lax.all_to_all(listed_keys, "ctx", split_axis=1, concat_axis=0, tiled=True),
        lax.all_to_all(listed_values, "ctx", split_axis=1, concat_axis=0, tiled=True),
    )
    tile_ids = jnp.arange(selected.shape[0], dtype=jnp.int32)[:, None]
    member = (selected.reshape(1, -1) == tile_ids).astype(jnp.bfloat16)
    entries = member.shape[1]
    sum_keys = jnp.dot(
        member, back_keys.reshape(entries, spread * columns), preferred_element_type=jnp.float32
    )
    sum_values = jnp.dot(
        member, back_values.reshape(entries, spread * columns), preferred_element_type=jnp.float32
    )
    held_key_grad = sum_keys.astype(jnp.bfloat16).reshape(devices, tiles_here, spread, columns)
    held_value_grad = sum_values.astype(jnp.bfloat16).reshape(devices, tiles_here, spread, columns)
    owned_keys, owned_values = (
        lax.all_to_all(held_key_grad, "ctx", split_axis=0, concat_axis=2, tiled=True),
        lax.all_to_all(held_value_grad, "ctx", split_axis=0, concat_axis=2, tiled=True),
    )
    grad_key = (
        owned_keys.reshape(height, columns).astype(jnp.float32)
        + jnp.repeat(own_coarse_keys, POOL, axis=0) / POOL
    ).astype(jnp.bfloat16)
    grad_value = (
        owned_values.reshape(height, columns).astype(jnp.float32)
        + jnp.repeat(own_coarse_values, POOL, axis=0) / POOL
    ).astype(jnp.bfloat16)
    attended = out_tiles[0]
    grad_query = query_tiles[0]
    return (attended, grad_query, grad_key, grad_value, own_coarse_keys, own_coarse_values)


def solution(mesh):
    in_specs = (
        P(("groups", "ctx"), None),
        P(("groups", "ctx"), None),
        P(("groups", "ctx"), None),
        P(("groups", "ctx"), None),
        P("groups", None),
    )
    out_specs = (
        P(("groups", "ctx"), None),
        P(("groups", "ctx"), None),
        P(("groups", "ctx"), None),
        P(("groups", "ctx"), None),
        P(("groups", "ctx"), None),
        P(("groups", "ctx"), None),
    )
    return jax.shard_map(shards, mesh=mesh, in_specs=in_specs, out_specs=out_specs, check_vma=False)
```

profile of v0, /device:TPU:1, one launch (start us, length us, event | category | flops | bytes accessed | tf_op | source)
XLA Modules:
  0.0 674.5 jit_solution(8619171968082053531)
XLA Ops:
  10.9 5.6 reduce.44
  17.8 7.7 %all-to-all-start.2 = ((bf16[16,2,12800]{2,1,0:T(2,128)(2,1)}), bf16[16,2,12800]{2,1,0:T(2,128)(2,1)}, u32[]{:S(2)}, u32[]{:S(2)}) async-start(bf16[16,2,12800]{2,1,0:T(2,128)(2,1)} %reshape.198), calls=%async_computation.2 | async-start | bytes 1638400 | tf_op jit(solution)/shard_map/all_to_all | solution.py:93
  27.7 5.6 reduce.45
  34.7 10.0 %all-to-all-done.2 = bf16[16,2,12800]{2,1,0:T(2,128)(2,1)} async-done(((bf16[16,2,12800]{2,1,0:T(2,128)(2,1)}), bf16[16,2,12800]{2,1,0:T(2,128)(2,1)}, u32[]{:S(2)}, u32[]{:S(2)}) %all-to-all-start.2) | async-done | bytes 819232 | tf_op jit(solution)/shard_map/all_to_all | solution.py:93
  44.7 6.2 all-to-all-start
  51.1 4.4 reshape.199
  55.6 5.6 bitcast_reduce_fusion.1
  62.5 3.3 gather_fusion.1
  65.8 4.3 all-to-all-done
  70.1 5.9 all-to-all-start.3
  76.0 4.4 reshape.201
  80.4 5.6 bitcast_reduce_fusion
  86.0 2.2 all_to_all.37
  89.3 3.2 gather_fusion
  92.6 79.7 %all-to-all-done.3 = bf16[16,8,8,2560]{3,2,1,0:T(8,128)(2,1)} async-done(((bf16[16,8,8,2560]{3,2,1,0:T(8,128)(2,1)}), bf16[16,8,8,2560]{3,2,1,0:T(8,128)(2,1)}, u32[]{:S(2)}, u32[]{:S(2)}) %all-to-all-start.3) | async-done | bytes 5242912 | tf_op jit(solution)/shard_map/all_to_all | solution.py:108
  172.2 23.5 %all-to-all-start.1 = ((bf16[16,8,8,2560]{3,2,1,0:T(8,128)(2,1)}), bf16[16,8,8,2560]{3,2,1,0:T(8,128)(2,1)}, u32[]{:S(2)}, u32[]{:S(2)}) async-start(bf16[16,8,8,2560]{3,2,1,0:T(8,128)(2,1)} %bitcast.197), calls=%async_computation.1 | async-start | bytes 10485760 | tf_op jit(solution)/shard_map/all_to_all | solution.py:107
  208.0 3.0 copy.67
  214.8 77.1 %all-to-all-done.1 = bf16[16,8,8,2560]{3,2,1,0:T(8,128)(2,1)} async-done(((bf16[16,8,8,2560]{3,2,1,0:T(8,128)(2,1)}), bf16[16,8,8,2560]{3,2,1,0:T(8,128)(2,1)}, u32[]{:S(2)}, u32[]{:S(2)}) %all-to-all-start.1) | async-done | bytes 5242912 | tf_op jit(solution)/shard_map/all_to_all | solution.py:107
  291.9 3.0 copy.65
  312.1 1.7 convolution_dynamic-update-slice_fusion.18
  315.5 1.7 convolution_dynamic-update-slice_fusion.16
  317.2 1.7 convolution_dynamic-update-slice_fusion.15
  319.0 1.8 convolution_dynamic-update-slice_fusion.14
  336.7 4.6 slice.832
  341.3 3.0 copy.91
  344.3 23.4 %all-to-all-start.6 = ((bf16[8,16,8,2560]{3,2,0,1:T(8,128)(2,1)}), bf16[8,16,8,2560]{3,2,0,1:T(8,128)(2,1)}, u32[]{:S(2)}, u32[]{:S(2)}) async-start(bf16[8,16,8,2560]{3,2,0,1:T(8,128)(2,1)} %copy.91), calls=%async_computation.6 | async-start | bytes 10485760 | tf_op jit(solution)/shard_map/all_to_all | solution.py:132
  367.8 2.2 constant_dynamic-update-slice_fusion.18
  370.8 2.1 constant_dynamic-update-slice_fusion.17
  372.9 2.1 constant_dynamic-update-slice_fusion.16
  422.5 4.6 slice.833
  427.1 2.8 copy.89
  430.0 34.1 %all-to-all-done.6 = bf16[8,16,8,2560]{3,2,0,1:T(8,128)(2,1)} async-done(((bf16[8,16,8,2560]{3,2,0,1:T(8,128)(2,1)}), bf16[8,16,8,2560]{3,2,0,1:T(8,128)(2,1)}, u32[]{:S(2)}, u32[]{:S(2)}) %all-to-all-start.6) | async-done | bytes 5242912 | tf_op jit(solution)/shard_map/all_to_all | solution.py:132
  464.1 23.3 %all-to-all-start.4 = ((bf16[8,16,8,2560]{3,2,0,1:T(8,128)(2,1)}), bf16[8,16,8,2560]{3,2,0,1:T(8,128)(2,1)}, u32[]{:S(2)}, u32[]{:S(2)}) async-start(bf16[8,16,8,2560]{3,2,0,1:T(8,128)(2,1)} %copy.89), calls=%async_computation.4 | async-start | bytes 10485760 | tf_op jit(solution)/shard_map/all_to_all | solution.py:131
  488.9 1.7 slice.441
  490.6 1.7 slice.439
  500.8 4.4 copy.119
  507.1 81.0 %all-to-all-done.4 = bf16[8,16,8,2560]{3,2,0,1:T(8,128)(2,1)} async-done(((bf16[8,16,8,2560]{3,2,0,1:T(8,128)(2,1)}), bf16[8,16,8,2560]{3,2,0,1:T(8,128)(2,1)}, u32[]{:S(2)}, u32[]{:S(2)}) %all-to-all-start.4) | async-done | bytes 5242912 | tf_op jit(solution)/shard_map/all_to_all | solution.py:131
  588.1 24.1 %all-to-all-start.7 = ((bf16[16,1,8,2560]{3,2,1,0:T(8,128)(2,1)}), bf16[16,1,8,2560]{3,2,1,0:T(8,128)(2,1)S(1)}, u32[]{:S(2)}, u32[]{:S(2)}) async-start(bf16[16,1,8,2560]{3,2,1,0:T(8,128)(2,1)} %bitcast.21), calls=%async_computation.7 | async-start | bytes 1310720 | tf_op jit(solution)/shard_map/all_to_all | solution.py:147
  612.2 2.0 fusion.87
  614.2 1.9 fusion.89
  618.0 4.4 copy.117
  624.3 4.8 all-to-all-done.7
  629.1 5.0 all-to-all-start.5
  634.2 2.0 fusion.95
  636.2 1.9 fusion.97
  639.1 2.2 copy.93
  642.2 2.2 copy.94
  644.4 19.7 %all-reduce.5.cloned.1.call-done = (f32[32,2560]{1,0:T(8,128)}, f32[32,2560]{1,0:T(8,128)}) async-done(((f32[32,2560]{1,0:T(8,128)}, f32[32,2560]{1,0:T(8,128)}), (f32[32,2560]{1,0:T(8,128)}, f32[32,2560]{1,0:T(8,128)})) %all-reduce.5.cloned.1.call-update) | async-done | bytes 655376
  (540 shorter events, 129.3 us)
Async XLA Ops:
  17.8 26.9 %all-to-all-start.2 = ((bf16[16,2,12800]{2,1,0:T(2,128)(2,1)}), bf16[16,2,12800]{2,1,0:T(2,128)(2,1)}, u32[]{:S(2)}, u32[]{:S(2)}) async-start(bf16[16,2,12800]{2,1,0:T(2,128)(2,1)} %reshape.198), calls=%async_computation.2 | async-start | bytes 1638400 | tf_op jit(solution)/shard_map/all_to_all | solution.py:93
  25.8 25.1 %copy-start.106 = (s32[16,8]{0,1:T(8,128)S(1)}, s32[16,8]{0,1:T(8,128)}, u32[]{:S(2)}) copy-start(s32[16,8]{0,1:T(8,128)} %param.9) | copy-start | bytes 1540
  44.7 25.4 %all-to-all-start = ((bf16[16,2,12800]{2,1,0:T(2,128)(2,1)}), bf16[16,2,12800]{2,1,0:T(2,128)(2,1)}, u32[]{:S(2)}, u32[]{:S(2)}) async-start(bf16[16,2,12800]{2,1,0:T(2,128)(2,1)} %reshape.200), calls=%async_computation | async-start | bytes 1638400 | tf_op jit(solution)/shard_map/all_to_all | solution.py:86
  70.1 102.1 %all-to-all-start.3 = ((bf16[16,8,8,2560]{3,2,1,0:T(8,128)(2,1)}), bf16[16,8,8,2560]{3,2,1,0:T(8,128)(2,1)}, u32[]{:S(2)}, u32[]{:S(2)}) async-start(bf16[16,8,8,2560]{3,2,1,0:T(8,128)(2,1)} %bitcast.198), calls=%async_computation.3 | async-start | bytes 10485760 | tf_op jit(solution)/shard_map/all_to_all | solution.py:108
  92.6 103.2 %slice-start.6 = ((bf16[128,2560]{1,0:T(8,128)(2,1)}), bf16[128,128]{1,0:T(8,128)(2,1)S(1)}, s32[]{:S(2)}) async-start(bf16[128,2560]{1,0:T(8,128)(2,1)} %param.8), calls=%async_computation.15 | async-start | bytes 65536
  92.6 103.9 %copy-start.70 = (bf16[128,2560]{1,0:T(8,128)(2,1)S(1)}, bf16[128,2560]{1,0:T(8,128)(2,1)}, u32[]{:S(2)}) copy-start(bf16[128,2560]{1,0:T(8,128)(2,1)} %param.8) | copy-start | bytes 1966084
  172.2 119.7 %all-to-all-start.1 = ((bf16[16,8,8,2560]{3,2,1,0:T(8,128)(2,1)}), bf16[16,8,8,2560]{3,2,1,0:T(8,128)(2,1)}, u32[]{:S(2)}, u32[]{:S(2)}) async-start(bf16[16,8,8,2560]{3,2,1,0:T(8,128)(2,1)} %bitcast.197), calls=%async_computation.1 | async-start | bytes 10485760 | tf_op jit(solution)/shard_map/all_to_all | solution.py:107
  297.4 16.4 %copy-start.27 = (f32[1056,128]{1,0:T(8,128)}, f32[1056,128]{1,0:T(8,128)S(1)}, u32[]{:S(2)}) copy-start(f32[1056,128]{1,0:T(8,128)S(1)} %get-tuple-element.78) | copy-start | bytes 1622020
  297.8 17.7 %copy-start.25 = (f32[1056,128]{1,0:T(8,128)}, f32[1056,128]{1,0:T(8,128)S(1)}, u32[]{:S(2)}) copy-start(f32[1056,128]{1,0:T(8,128)S(1)} %get-tuple-element.82) | copy-start | bytes 1622020
  297.8 17.7 %copy-start.119 = (f32[128]{0:T(128)}, f32[128]{0:T(128)S(1)}, u32[]{:S(2)}) copy-start(f32[128]{0:T(128)S(1)} %get-tuple-element.81) | copy-start | bytes 1540
  298.1 19.1 %copy-start.23 = (f32[1056,128]{1,0:T(8,128)}, f32[1056,128]{1,0:T(8,128)S(1)}, u32[]{:S(2)}) copy-start(f32[1056,128]{1,0:T(8,128)S(1)} %get-tuple-element.86) | copy-start | bytes 1622020
  298.1 19.1 %copy-start.117 = (f32[128]{0:T(128)}, f32[128]{0:T(128)S(1)}, u32[]{:S(2)}) copy-start(f32[128]{0:T(128)S(1)} %get-tuple-element.85) | copy-start | bytes 1540
  298.4 20.5 %copy-start.21 = (f32[1056,128]{1,0:T(8,128)}, f32[1056,128]{1,0:T(8,128)S(1)}, u32[]{:S(2)}) copy-start(f32[1056,128]{1,0:T(8,128)S(1)} %get-tuple-element.90) | copy-start | bytes 1622020
  298.5 20.5 %copy-start.115 = (f32[128]{0:T(128)}, f32[128]{0:T(128)S(1)}, u32[]{:S(2)}) copy-start(f32[128]{0:T(128)S(1)} %get-tuple-element.89) | copy-start | bytes 1540
  298.8 22.0 %copy-start.19 = (f32[1056,128]{1,0:T(8,128)}, f32[1056,128]{1,0:T(8,128)S(1)}, u32[]{:S(2)}) copy-start(f32[1056,128]{1,0:T(8,128)S(1)} %get-tuple-element.94) | copy-start | bytes 1622020
  298.8 22.0 %copy-start.113 = (f32[128]{0:T(128)}, f32[128]{0:T(128)S(1)}, u32[]{:S(2)}) copy-start(f32[128]{0:T(128)S(1)} %get-tuple-element.93) | copy-start | bytes 1540
  299.1 22.8 %copy-start.17 = (f32[1056,128]{1,0:T(8,128)}, f32[1056,128]{1,0:T(8,128)S(1)}, u32[]{:S(2)}) copy-start(f32[1056,128]{1,0:T(8,128)S(1)} %get-tuple-element.98) | copy-start | bytes 1622020
  299.1 22.8 %copy-start.111 = (f32[128]{0:T(128)}, f32[128]{0:T(128)S(1)}, u32[]{:S(2)}) copy-start(f32[128]{0:T(128)S(1)} %get-tuple-element.97) | copy-start | bytes 1540
  299.4 23.6 %copy-start.15 = (f32[1056,128]{1,0:T(8,128)}, f32[1056,128]{1,0:T(8,128)S(1)}, u32[]{:S(2)}) copy-start(f32[1056,128]{1,0:T(8,128)S(1)} %get-tuple-element.102) | copy-start | bytes 1622020
  299.4 23.6 %copy-start.109 = (f32[128]{0:T(128)}, f32[128]{0:T(128)S(1)}, u32[]{:S(2)}) copy-start(f32[128]{0:T(128)S(1)} %get-tuple-element.101) | copy-start | bytes 1540
  299.8 24.3 %copy-start.13 = (f32[1056,128]{1,0:T(8,128)}, f32[1056,128]{1,0:T(8,128)S(1)}, u32[]{:S(2)}) copy-start(f32[1056,128]{1,0:T(8,128)S(1)} %get-tuple-element.106) | copy-start | bytes 1622020
  299.8 24.3 %copy-start.107 = (f32[128]{0:T(128)}, f32[128]{0:T(128)S(1)}, u32[]{:S(2)}) copy-start(f32[128]{0:T(128)S(1)} %get-tuple-element.105) | copy-start | bytes 1540
  300.1 25.5 %copy-start.11 = (f32[1056,128]{1,0:T(8,128)}, f32[1056,128]{1,0:T(8,128)S(1)}, u32[]{:S(2)}) copy-start(f32[1056,128]{1,0:T(8,128)S(1)} %get-tuple-element.110) | copy-start | bytes 1622020
  300.4 26.3 %copy-start.9 = (f32[1056,128]{1,0:T(8,128)}, f32[1056,128]{1,0:T(8,128)S(1)}, u32[]{:S(2)}) copy-start(f32[1056,128]{1,0:T(8,128)S(1)} %get-tuple-element.114) | copy-start | bytes 1622020
  300.7 27.0 %copy-start.7 = (f32[1056,128]{1,0:T(8,128)}, f32[1056,128]{1,0:T(8,128)S(1)}, u32[]{:S(2)}) copy-start(f32[1056,128]{1,0:T(8,128)S(1)} %get-tuple-element.118) | copy-start | bytes 1622020
  301.1 27.8 %copy-start.5 = (f32[1056,128]{1,0:T(8,128)}, f32[1056,128]{1,0:T(8,128)S(1)}, u32[]{:S(2)}) copy-start(f32[1056,128]{1,0:T(8,128)S(1)} %get-tuple-element.122) | copy-start | bytes 1622020
  301.4 28.6 %copy-start.3 = (f32[1056,128]{1,0:T(8,128)}, f32[1056,128]{1,0:T(8,128)S(1)}, u32[]{:S(2)}) copy-start(f32[1056,128]{1,0:T(8,128)S(1)} %get-tuple-element.126) | copy-start | bytes 1622020
  303.0 32.6 %copy-start.31 = (f32[1056,128]{1,0:T(8,128)}, f32[1056,128]{1,0:T(8,128)S(1)}, u32[]{:S(2)}) copy-start(f32[1056,128]{1,0:T(8,128)S(1)} %get-tuple-element.146) | copy-start | bytes 1622020
  303.0 32.6 %copy-start.125 = (f32[128]{0:T(128)}, f32[128]{0:T(128)S(1)}, u32[]{:S(2)}) copy-start(f32[128]{0:T(128)S(1)} %get-tuple-element.145) | copy-start | bytes 1540
  306.4 29.2 %copy-start.127 = (f32[128]{0:T(128)}, f32[128]{0:T(128)S(1)}, u32[]{:S(2)}) copy-start(f32[128]{0:T(128)S(1)} %fusion.141) | copy-start | bytes 1540
  311.1 16.7 %copy-start.141 = (f32[128]{0:T(128)}, f32[128]{0:T(128)S(1)}, u32[]{:S(2)}) copy-start(f32[128]{0:T(128)S(1)} %fusion.127) | copy-start | bytes 1540
  311.2 17.6 %copy-start.139 = (f32[128]{0:T(128)}, f32[128]{0:T(128)S(1)}, u32[]{:S(2)}) copy-start(f32[128]{0:T(128)S(1)} %fusion.129) | copy-start | bytes 1540
  311.4 18.6 %copy-start.137 = (f32[128]{0:T(128)}, f32[128]{0:T(128)S(1)}, u32[]{:S(2)}) copy-start(f32[128]{0:T(128)S(1)} %fusion.131) | copy-start | bytes 1540
  311.6 19.5 %copy-start.135 = (f32[128]{0:T(128)}, f32[128]{0:T(128)S(1)}, u32[]{:S(2)}) copy-start(f32[128]{0:T(128)S(1)} %fusion.133) | copy-start | bytes 1540
  311.7 20.5 %copy-start.133 = (f32[128]{0:T(128)}, f32[128]{0:T(128)S(1)}, u32[]{:S(2)}) copy-start(f32[128]{0:T(128)S(1)} %fusion.135) | copy-start | bytes 1540
  311.9 21.4 %copy-start.131 = (f32[128]{0:T(128)}, f32[128]{0:T(128)S(1)}, u32[]{:S(2)}) copy-start(f32[128]{0:T(128)S(1)} %fusion.137) | copy-start | bytes 1540
  312.1 22.4 %copy-start.129 = (f32[128]{0:T(128)}, f32[128]{0:T(128)S(1)}, u32[]{:S(2)}) copy-start(f32[128]{0:T(128)S(1)} %fusion.139) | copy-start | bytes 1540
  344.3 28.6 %copy-start.104 = (bf16[128,128]{0,1:T(8,128)(2,1)S(1)}, bf16[128,128]{0,1:T(8,128)(2,1)}, u32[]{:S(2)}) copy-start(bf16[128,128]{0,1:T(8,128)(2,1)} %copy.99) | copy-start | bytes 98308
  344.3 119.8 %all-to-all-start.6 = ((bf16[8,16,8,2560]{3,2,0,1:T(8,128)(2,1)}), bf16[8,16,8,2560]{3,2,0,1:T(8,128)(2,1)}, u32[]{:S(2)}, u32[]{:S(2)}) async-start(bf16[8,16,8,2560]{3,2,0,1:T(8,128)(2,1)} %copy.91), calls=%async_computation.6 | async-start | bytes 10485760 | tf_op jit(solution)/shard_map/all_to_all | solution.py:132
  430.0 57.7 %copy-start.155 = (u32[32]{0:T(128)S(1)}, u32[32]{0:T(128)}, u32[]{:S(2)}) copy-start(u32[32]{0:T(128)} %constant.21) | copy-start | bytes 388
  430.0 62.4 %copy-start.34 = (bf16[1056,128]{1,0:T(8,128)(2,1)S(1)}, bf16[1056,128]{1,0:T(8,128)(2,1)}, u32[]{:S(2)}) copy-start(bf16[1056,128]{1,0:T(8,128)(2,1)} %fusion.59) | copy-start | bytes 811012
  464.1 124.0 %all-to-all-start.4 = ((bf16[8,16,8,2560]{3,2,0,1:T(8,128)(2,1)}), bf16[8,16,8,2560]{3,2,0,1:T(8,128)(2,1)}, u32[]{:S(2)}, u32[]{:S(2)}) async-start(bf16[8,16,8,2560]{3,2,0,1:T(8,128)(2,1)} %copy.89), calls=%async_computation.4 | async-start | bytes 10485760 | tf_op jit(solution)/shard_map/all_to_all | solution.py:131
  487.4 176.6 %all-reduce.5.cloned.1.call-start = ((), (), s32[]{:S(2)}) async-start(), calls=%async_computation.8 | async-start | bytes 1310720
  505.2 106.9 %copy-start.52 = (bf16[1056,128]{1,0:T(8,128)(2,1)S(1)}, bf16[1056,128]{1,0:T(8,128)(2,1)}, u32[]{:S(2)}) copy-start(bf16[1056,128]{1,0:T(8,128)(2,1)} %copy-done.51) | copy-start | bytes 811012
  506.0 108.2 %copy-start.56 = (bf16[1056,128]{1,0:T(8,128)(2,1)S(1)}, bf16[1056,128]{1,0:T(8,128)(2,1)}, u32[]{:S(2)}) copy-start(bf16[1056,128]{1,0:T(8,128)(2,1)} %copy-done.55) | copy-start | bytes 811012
  588.1 28.0 %slice-start.2 = ((s8[5242880]{0:T(1024)(128)(4,1)}), s8[1048576]{0:T(1024)(128)(4,1)S(1)}, s32[]{:S(2)}) async-start(s8[5242880]{0:T(1024)(128)(4,1)} %bitcast.187), calls=%async_computation.11 | async-start | bytes 2097152
  588.1 41.0 %all-to-all-start.7 = ((bf16[16,1,8,2560]{3,2,1,0:T(8,128)(2,1)}), bf16[16,1,8,2560]{3,2,1,0:T(8,128)(2,1)S(1)}, u32[]{:S(2)}, u32[]{:S(2)}) async-start(bf16[16,1,8,2560]{3,2,1,0:T(8,128)(2,1)} %bitcast.21), calls=%async_computation.7 | async-start | bytes 1310720 | tf_op jit(solution)/shard_map/all_to_all | solution.py:147
  629.1 37.4 %all-to-all-start.5 = ((bf16[16,1,8,2560]{3,2,1,0:T(8,128)(2,1)}), bf16[16,1,8,2560]{3,2,1,0:T(8,128)(2,1)S(1)}, u32[]{:S(2)}, u32[]{:S(2)}) async-start(bf16[16,1,8,2560]{3,2,1,0:T(8,128)(2,1)} %bitcast.15), calls=%async_computation.5 | async-start | bytes 1310720 | tf_op jit(solution)/shard_map/all_to_all | solution.py:146
  (124 other events, 698.0 us)
Sparse Core Ops, SparseCore 0:
  492.5 171.5 all-reduce.4
where the time goes:
time: 682 us; the launch traced here: 675 us
  waiting for transfers between devices  311 us (46%)
  starting transfers between devices  119 us (17%)
  matrix products  105 us (15%)
  local copies, waits for them, and re-layouts  92.8 us (14%)
  other arithmetic  29.9 us (4%)
  between operations  16.6 us (2%)
    all_to_all x1, waiting for transfers between devices, shards(): lax.all_to_all(listed_keys, 'ctx', split_axis=1, concat_axis=0, tiled=True)  81 us
    all_to_all x1, waiting for transfers between devices, shards(): lax.all_to_all(held_values[selected], 'ctx', split_axis=0, concat_axis=2,...  79.7 us
    all_to_all x1, waiting for transfers between devices, shards(): lax.all_to_all(held_keys[selected], 'ctx', split_axis=0, concat_axis=2, t...  77.1 us
    dot_general x80, matrix products, contract(): lax.dot_general(left, right, (((left_dim,), (right_dim,)), ((), ())), pre...  62.3 us
    unnamed x360, local copies, waits for them, and re-layouts  43 us
    all_to_all x1, waiting for transfers between devices, shards(): lax.all_to_all(listed_values, 'ctx', split_axis=1, concat_axis=0, tiled=T...  34.1 us
    all_to_all x1, starting transfers between devices, shards(): lax.all_to_all(held_value_grad, 'ctx', split_axis=0, concat_axis=2, tiled...  24.1 us
    dot_general x20, matrix products, attend(): jnp.dot(rounded, head_value, preferred_element_type=jnp.float32)  23.7 us
  transfers between devices with their start and end apart: 9, of which 8 were waited for; matrix products, arithmetic and copies ran while one was open for 23% of the time, Pallas kernels for 0%

commit v1 on v0

--- a/solution.py
+++ b/solution.py
@@ -1,6 +1,10 @@
+import functools
+
 import jax
 import jax.numpy as jnp
 from jax import lax
+from jax.experimental import pallas as pl
+from jax.experimental.pallas import tpu as pltpu
 from jax.sharding import PartitionSpec as P
 
 HEADS = 20
@@ -73,7 +77,7 @@
     )
 
 
-def shards(query_rows, key_rows, value_rows, out_grad, selected):
+def listed_shards(query_rows, key_rows, value_rows, out_grad, selected):
     height, columns = query_rows.shape
     devices = lax.axis_size("ctx")
     tiles_here = height // TILE
@@ -159,6 +163,403 @@
     return (attended, grad_query, grad_key, grad_value, own_coarse_keys, own_coarse_values)
 
 
+LANES = 128
+SPLITS = 3
+VMEM = pl.BlockSpec(memory_space=pltpu.VMEM)
+SMEM = pl.BlockSpec(memory_space=pltpu.SMEM)
+BIG = pltpu.CompilerParams(vmem_limit_bytes=50 * 1024 * 1024)
+
+
+def nt(left, right):
+    return contract(left, right, 1, 1)
+
+
+def nn(left, right):
+    return contract(left, right, 1, 0)
+
+
+def split_rows(total):
+    parts = []
+    for _ in range(SPLITS):
+        part = total.astype(jnp.bfloat16)
+        parts.append(part.astype(jnp.float32))
+        total = total - parts[-1]
+    return parts
+
+
+def tail_rows(coarse_key, coarse_value):
+    per_tile = TILE // POOL
+    parts = split_rows(jnp.concatenate([coarse_key, coarse_value], axis=0))
+    used = SPLITS * 2 * per_tile
+    filler = jnp.zeros((tail_height() - used, LANES), jnp.float32)
+    return jnp.concatenate(parts + [filler], axis=0).astype(jnp.bfloat16)
+
+
+def tail_height():
+    used = SPLITS * 2 * (TILE // POOL)
+    return -(-used // 16) * 16
+
+
+def join_tail(tail):
+    pair = 2 * (TILE // POOL)
+    rows = tail.astype(jnp.float32)
+    total = rows[:pair]
+    for part in range(1, SPLITS):
+        total = total + rows[part * pair : (part + 1) * pair]
+    return total
+
+
+def pack_body(q_ref, k_ref, v_ref, g_ref, out_ref):
+    for place in range(out_ref.shape[0]):
+        columns = slice(place * LANES, (place + 1) * LANES)
+        for index, ref in enumerate((q_ref, k_ref, v_ref, g_ref)):
+            out_ref[place, index * TILE : (index + 1) * TILE, :] = ref[:, columns]
+
+
+def pack(arrays, first, count, step):
+    spec = pl.BlockSpec((TILE, step * LANES), lambda i: (0, first // step + i))
+    return pl.pallas_call(
+        pack_body,
+        grid=(count // step,),
+        in_specs=[spec] * 4,
+        out_specs=pl.BlockSpec((step, 4 * TILE, LANES), lambda i: (i, 0, 0)),
+        out_shape=jax.ShapeDtypeStruct((count, 4 * TILE, LANES), jnp.bfloat16),
+        name="pack",
+    )(*arrays)
+
+
+def prepare(tiles, get_key, get_value, scratch):
+    pool_key, pool_value, key_t, value_t, key_sum, value_sum = scratch
+    per_tile = TILE // POOL
+
+    def one(tile, carry):
+        for get, pool_ref, flip_ref in (
+            (get_key, pool_key, key_t),
+            (get_value, pool_value, value_t),
+        ):
+            rows = get(tile).astype(jnp.float32)
+            means = [
+                jnp.mean(rows[part * POOL : (part + 1) * POOL], axis=0, keepdims=True)
+                for part in range(per_tile)
+            ]
+            pool_ref[pl.ds(tile * per_tile, per_tile), :] = jnp.concatenate(means, axis=0)
+            flip_ref[tile] = rows.T.astype(jnp.bfloat16)
+        key_sum[tile] = jnp.zeros((TILE, LANES), jnp.float32)
+        value_sum[tile] = jnp.zeros((TILE, LANES), jnp.float32)
+        return carry
+
+    lax.fori_loop(0, tiles, one, 0)
+
+
+def one_tile(query, grad, listed, get_key, get_value, scratch, work):
+    pool_key, pool_value, key_t, value_t, key_sum, value_sum, pool_key_sum, pool_value_sum = scratch
+    score_ref, round_ref, slope_ref = work
+    scaling = HEAD_DIM ** (-0.5)
+    base2 = scaling * 1.4426950408889634
+    comp = pool_key.shape[0]
+    coarse_key = pool_key[...].astype(jnp.bfloat16)
+    coarse_value = pool_value[...].astype(jnp.bfloat16)
+    spans = [(slot * TILE, TILE) for slot in range(SEL)] + [(SEL * TILE, comp)]
+    keys = [get_key(tile) for tile in listed] + [coarse_key]
+    top = None
+    for (start, size), key in zip(spans, keys):
+        score = nt(key, query)
+        score_ref[start : start + size, :] = score
+        peak = jnp.max(score, axis=0, keepdims=True)
+        top = peak if top is None else jnp.maximum(top, peak)
+    total = jnp.zeros((1, LANES), jnp.float32)
+    for start, size in spans:
+        raised = jnp.exp2((score_ref[start : start + size, :] - top) * base2)
+        score_ref[start : start + size, :] = raised
+        total = total + jnp.sum(raised, axis=0, keepdims=True)
+    inverse = 1.0 / total
+    for start, size in spans:
+        weight = score_ref[start : start + size, :] * inverse
+        score_ref[start : start + size, :] = weight
+        round_ref[start : start + size, :] = weight.astype(jnp.bfloat16)
+    values_t = jnp.concatenate([value_t[tile] for tile in listed], axis=1)
+    out_t = nn(values_t, round_ref[: SEL * TILE, :]) + contract(
+        coarse_value, round_ref[SEL * TILE :, :], 0, 0
+    )
+    out_t = out_t.astype(jnp.bfloat16).astype(jnp.float32)
+    grad_t = grad.astype(jnp.float32).T
+    dots = jnp.sum(out_t * grad_t, axis=0, keepdims=True)
+    values = [get_value(tile) for tile in listed] + [coarse_value]
+    for place, ((start, size), value) in enumerate(zip(spans, values)):
+        slope = (score_ref[start : start + size, :] * (nt(value, grad) - dots)).astype(jnp.bfloat16)
+        slope_ref[start : start + size, :] = slope
+        key_term = nn(slope, query)
+        value_term = nn(round_ref[start : start + size, :], grad)
+        if place < SEL:
+            key_sum[listed[place]] += key_term
+            value_sum[listed[place]] += value_term
+        else:
+            pool_key_sum[...] += key_term
+            pool_value_sum[...] += value_term
+    keys_t = jnp.concatenate([key_t[tile] for tile in listed], axis=1)
+    query_t = nn(keys_t, slope_ref[: SEL * TILE, :]) + contract(
+        coarse_key, slope_ref[SEL * TILE :, :], 0, 0
+    )
+    return out_t.T.astype(jnp.bfloat16), (query_t.T * scaling).astype(jnp.bfloat16)
+
+
+def finish(tile, scratch):
+    scaling = HEAD_DIM ** (-0.5)
+    key_sum, value_sum, pool_key_sum, pool_value_sum = scratch
+    per_tile = TILE // POOL
+    coarse_key = pool_key_sum[pl.ds(tile * per_tile, per_tile), :] * scaling
+    coarse_value = pool_value_sum[pl.ds(tile * per_tile, per_tile), :]
+
+    def whole(fine, coarse):
+        return jnp.concatenate(
+            [
+                fine[part * POOL : (part + 1) * POOL] + coarse[part : part + 1] * (1.0 / POOL)
+                for part in range(per_tile)
+            ],
+            axis=0,
+        )
+
+    return (
+        whole(key_sum[tile] * scaling, coarse_key),
+        whole(value_sum[tile], coarse_value),
+        coarse_key,
+        coarse_value,
+    )
+
+
+def head_scratch(tiles):
+    comp = tiles * (TILE // POOL)
+    return [
+        pltpu.VMEM((comp, LANES), jnp.float32),
+        pltpu.VMEM((comp, LANES), jnp.float32),
+        pltpu.VMEM((tiles, LANES, TILE), jnp.bfloat16),
+        pltpu.VMEM((tiles, LANES, TILE), jnp.bfloat16),
+        pltpu.VMEM((tiles, TILE, LANES), jnp.float32),
+        pltpu.VMEM((tiles, TILE, LANES), jnp.float32),
+        pltpu.VMEM((comp, LANES), jnp.float32),
+        pltpu.VMEM((comp, LANES), jnp.float32),
+        pltpu.VMEM((SEL * TILE + comp, LANES), jnp.float32),
+        pltpu.VMEM((SEL * TILE + comp, LANES), jnp.bfloat16),
+        pltpu.VMEM((SEL * TILE + comp, LANES), jnp.bfloat16),
+    ]
+
+
+def whole_head(sel_ref, in_ref, out_ref, *scratch):
+    tiles = in_ref.shape[0]
+    totals, work = scratch[:8], scratch[8:]
+
+    def get_key(tile):
+        return in_ref[tile, TILE : 2 * TILE, :]
+
+    def get_value(tile):
+        return in_ref[tile, 2 * TILE : 3 * TILE, :]
+
+    prepare(tiles, get_key, get_value, totals[:6])
+    totals[6][...] = jnp.zeros_like(totals[6])
+    totals[7][...] = jnp.zeros_like(totals[7])
+
+    def one(tile, carry):
+        listed = [sel_ref[tile, slot] for slot in range(SEL)]
+        rows, slopes = one_tile(
+            in_ref[tile, :TILE, :],
+            in_ref[tile, 3 * TILE :, :],
+            listed,
+            get_key,
+            get_value,
+            totals,
+            work,
+        )
+        out_ref[tile, :TILE, :] = rows
+        out_ref[tile, TILE : 2 * TILE, :] = slopes
+        return carry
+
+    lax.fori_loop(0, tiles, one, 0)
+
+    def last(tile, carry):
+        key, value, coarse_key, coarse_value = finish(tile, totals[4:])
+        out_ref[tile, 2 * TILE : 3 * TILE, :] = key.astype(jnp.bfloat16)
+        out_ref[tile, 3 * TILE : 4 * TILE, :] = value.astype(jnp.bfloat16)
+        out_ref[tile, 4 * TILE :, :] = tail_rows(coarse_key, coarse_value)
+        return carry
+
+    lax.fori_loop(0, tiles, last, 0)
+
+
+def shared_head(span, planes, place_ref, sel_ref, own_ref, *refs):
+    pieces = refs[: span - 1]
+    out_ref, keep_ref = refs[span - 1 : span + 1]
+    send_refs = refs[span + 1 : 2 * span]
+    keys, values = refs[2 * span : 2 * span + 2]
+    scratch = refs[2 * span + 2 :]
+    totals, work = scratch[:8], scratch[8:]
+    tiles = span * planes
+    place = place_ref[0]
+    for step in range(span):
+        for plane in range(planes):
+            tile = plane * span + lax.bitwise_xor(place, step)
+            if step == 0:
+                keys[tile] = own_ref[plane, TILE : 2 * TILE, :]
+                values[tile] = own_ref[plane, 2 * TILE : 3 * TILE, :]
+            else:
+                keys[tile] = pieces[step - 1][plane, :TILE, :]
+                values[tile] = pieces[step - 1][plane, TILE:, :]
+
+    def get_key(tile):
+        return keys[tile]
+
+    def get_value(tile):
+        return values[tile]
+
+    prepare(tiles, get_key, get_value, totals[:6])
+    totals[6][...] = jnp.zeros_like(totals[6])
+    totals[7][...] = jnp.zeros_like(totals[7])
+
+    def one(plane, carry):
+        listed = [sel_ref[plane * span + place, slot] for slot in range(SEL)]
+        rows, slopes = one_tile(
+            own_ref[plane, :TILE, :],
+            own_ref[plane, 3 * TILE :, :],
+            listed,
+            get_key,
+            get_value,
+            totals,
+            work,
+        )
+        out_ref[plane, :TILE, :] = rows
+        out_ref[plane, TILE:, :] = slopes
+        return carry
+
+    lax.fori_loop(0, planes, one, 0)
+    for step in range(span):
+        def last(plane, carry, step=step):
+            tile = plane * span + lax.bitwise_xor(place, step)
+            key, value, coarse_key, coarse_value = finish(tile, totals[4:])
+            if step == 0:
+                pair = 2 * (TILE // POOL)
+                keep_ref[plane, :TILE, :] = key
+                keep_ref[plane, TILE : 2 * TILE, :] = value
+                keep_ref[plane, 2 * TILE : 2 * TILE + 8, :] = jnp.concatenate(
+                    [coarse_key, coarse_value, jnp.zeros((8 - pair, LANES), jnp.float32)], axis=0
+                )
+            else:
+                ref = send_refs[step - 1]
+                ref[plane, :TILE, :] = key.astype(jnp.bfloat16)
+                ref[plane, TILE : 2 * TILE, :] = value.astype(jnp.bfloat16)
+                ref[plane, 2 * TILE :, :] = tail_rows(coarse_key, coarse_value)
+            return carry
+
+        lax.fori_loop(0, planes, last, 0)
+
+
+def gather_terms(span, rows_ref, keep_ref, *refs):
+    pieces, out_ref = refs[: span - 1], refs[span - 1]
+    per_tile = TILE // POOL
+
+    def one(plane, carry):
+        fine = keep_ref[plane, : 2 * TILE, :]
+        coarse = keep_ref[plane, 2 * TILE : 2 * TILE + 2 * per_tile, :]
+        for piece in pieces:
+            fine = fine + piece[plane, : 2 * TILE, :].astype(jnp.float32)
+            coarse = coarse + join_tail(piece[plane, 2 * TILE :, :])
+        out_ref[plane, : 2 * TILE, :] = rows_ref[plane]
+        out_ref[plane, 2 * TILE : 4 * TILE, :] = fine.astype(jnp.bfloat16)
+        out_ref[plane, 4 * TILE :, :] = tail_rows(coarse[:per_tile], coarse[per_tile:])
+        return carry
+
+    lax.fori_loop(0, rows_ref.shape[0], one, 0)
+
+
+def unpack_body(main_ref, rest_ref, a_ref, q_ref, k_ref, v_ref, pk_ref, pv_ref):
+    per_tile = TILE // POOL
+    heads = main_ref.shape[0]
+    for head in range(heads + rest_ref.shape[0]):
+        ref, place = (main_ref, head) if head < heads else (rest_ref, head - heads)
+        columns = slice(head * LANES, (head + 1) * LANES)
+        for index, out in enumerate((a_ref, q_ref, k_ref, v_ref)):
+            out[:, columns] = ref[place, index * TILE : (index + 1) * TILE, :]
+        coarse = join_tail(ref[place, 4 * TILE :, :])
+        pk_ref[:, columns] = coarse[:per_tile]
+        pv_ref[:, columns] = coarse[per_tile:]
+
+
+def head_shards(query_rows, key_rows, value_rows, out_grad, selected):
+    devices = lax.axis_size("ctx")
+    height, columns = query_rows.shape
+    planes = HEADS - devices
+    span = devices // planes
+    arrays = (query_rows, key_rows, value_rows, out_grad)
+    place = jnp.reshape(lax.axis_index("ctx") % span, (1,))
+    columns_of = [[p * span + w for p in range(planes)] for w in range(span)]
+
+    def shift(block, step):
+        return lax.ppermute(block, "ctx", [(i, i ^ step) for i in range(devices)])
+
+    def swap(block, groups=None):
+        return lax.all_to_all(block, "ctx", 0, 0, axis_index_groups=groups, tiled=True)
+
+    block = 4 * TILE + tail_height()
+    part = 2 * TILE + tail_height()
+    own = swap(pack(arrays, devices, planes, planes), columns_of)
+    main = swap(pack(arrays, 0, devices, 4))
+    own_kv = own[:, TILE : 3 * TILE, :]
+    pieces = [shift(own_kv, step) for step in range(1, span)]
+    outs = pl.pallas_call(
+        functools.partial(shared_head, span, planes),
+        in_specs=[SMEM, SMEM] + [VMEM] * span,
+        out_specs=[VMEM] * (span + 1),
+        out_shape=[
+            jax.ShapeDtypeStruct((planes, 2 * TILE, LANES), jnp.bfloat16),
+            jax.ShapeDtypeStruct((planes, 2 * TILE + 8, LANES), jnp.float32),
+        ]
+        + [jax.ShapeDtypeStruct((planes, part, LANES), jnp.bfloat16)] * (span - 1),
+        scratch_shapes=[pltpu.VMEM((devices, TILE, LANES), jnp.bfloat16)] * 2
+        + head_scratch(devices),
+        compiler_params=BIG,
+        name="shared_head",
+    )(place, selected, own, *pieces)
+    terms = [shift(sent, step + 1) for step, sent in enumerate(outs[2:])]
+    rest = pl.pallas_call(
+        functools.partial(gather_terms, span),
+        in_specs=[VMEM] * (span + 1),
+        out_specs=VMEM,
+        out_shape=jax.ShapeDtypeStruct((planes, block, LANES), jnp.bfloat16),
+        compiler_params=BIG,
+        name="gather_terms",
+    )(outs[0], outs[1], *terms)
+    rest = swap(rest, columns_of)
+    done = pl.pallas_call(
+        whole_head,
+        in_specs=[SMEM, VMEM],
+        out_specs=VMEM,
+        out_shape=jax.ShapeDtypeStruct((devices, block, LANES), jnp.bfloat16),
+        scratch_shapes=head_scratch(devices),
+        compiler_params=BIG,
+        name="whole_head",
+    )(selected, main)
+    done = swap(done)
+    wide = jax.ShapeDtypeStruct((height, columns), jnp.bfloat16)
+    thin = jax.ShapeDtypeStruct((height // POOL, columns), jnp.float32)
+    return pl.pallas_call(
+        unpack_body,
+        in_specs=[VMEM, VMEM],
+        out_specs=[VMEM] * 6,
+        out_shape=[wide, wide, wide, wide, thin, thin],
+        compiler_params=BIG,
+        name="unpack",
+    )(done, rest)
+
+
+def shards(query_rows, key_rows, value_rows, out_grad, selected):
+    devices = lax.axis_size("ctx")
+    planes = HEADS - devices
+    tiles_here = query_rows.shape[0] // TILE
+    if planes > 0 and devices % planes == 0 and tiles_here == 1:
+        span = devices // planes
+        if span & (span - 1) == 0:
+            return head_shards(query_rows, key_rows, value_rows, out_grad, selected)
+    return listed_shards(query_rows, key_rows, value_rows, out_grad, selected)
+
+
 def solution(mesh):
     in_specs = (
         P(("groups", "ctx"), None),

time: 682 us -> 178 us (0.26); the launches traced: 675 us -> 177 us
  waiting for transfers between devices: 311 us -> 51.5 us
  matrix products: 105 us -> 0 us
  starting transfers between devices: 119 us -> 21.5 us
  local copies, waits for them, and re-layouts: 92.8 us -> 0.79 us
  blocking collectives: 0 us -> 58.3 us
  Pallas kernels: 0 us -> 44.7 us
  other arithmetic: 29.9 us -> 0 us
  between operations: 16.6 us -> 0.65 us
    all_to_all x8 -> x3, waiting for transfers between devices: 291 us -> 10.1 us  [swap(): lax.all_to_all(block, 'ctx', 0, 0, axis_index_groups=groups, tiled=True)]
    dot_general x122 -> x0, matrix products: 105 us -> none  [the longest x80 62.3 us: contract(): lax.dot_general(left, right, (((left_dim,), (right_dim,)), ((), ())), pre...]
    all_to_all x8 -> x3, starting transfers between devices: 119 us -> 16.5 us  [swap(): lax.all_to_all(block, 'ctx', 0, 0, axis_index_groups=groups, tiled=True)]
    all_to_all x0 -> x1, blocking collectives: none -> 58.3 us  [swap(): lax.all_to_all(block, 'ctx', 0, 0, axis_index_groups=groups, tiled=True)]
    pallas_call x0 -> x6, Pallas kernels: none -> 44.7 us  [the longest x1 27.2 us: head_shards(): pl.pallas_call(whole_head, in_specs=[SMEM, VMEM], out_specs=VMEM, out_sha...]
    unnamed x360 -> x3, local copies, waits for them, and re-layouts: 43 us -> 0.07 us
    ppermute x0 -> x6, waiting for transfers between devices: none -> 41.4 us  [shift(): return lax.ppermute(block, 'ctx', [(i, i ^ step) for i in range(devices)])]
    all_to_all x6 -> x0, local copies, waits for them, and re-layouts: 20.6 us -> none  [the longest x2 7.78 us: shards(): lax.all_to_all(package(key_tiles, own_keys, devices, spread), 'ctx', spli...]
  transfers between devices with their start and end apart: 9 -> 9, of which waited for: 8 -> 5; matrix products, arithmetic and copies ran while one was open for 23% -> 0% of each run, Pallas kernels for 0% -> 23%
where the time goes in v1:
time: 178 us; the launch traced here: 177 us
  blocking collectives  58.3 us (33%)
  waiting for transfers between devices  51.5 us (29%)
  Pallas kernels  44.7 us (25%)
  starting transfers between devices  21.5 us (12%)
    all_to_all x1, blocking collectives, swap(): lax.all_to_all(block, 'ctx', 0, 0, axis_index_groups=groups, tiled=True)  58.3 us
    ppermute x6, waiting for transfers between devices, shift(): return lax.ppermute(block, 'ctx', [(i, i ^ step) for i in range(devices)])  41.4 us
    pallas_call x1, Pallas kernels, head_shards(): pl.pallas_call(whole_head, in_specs=[SMEM, VMEM], out_specs=VMEM, out_sha...  27.2 us
    all_to_all x3, starting transfers between devices, swap(): lax.all_to_all(block, 'ctx', 0, 0, axis_index_groups=groups, tiled=True)  16.5 us
    all_to_all x3, waiting for transfers between devices, swap(): lax.all_to_all(block, 'ctx', 0, 0, axis_index_groups=groups, tiled=True)  10.1 us
    pallas_call x1, Pallas kernels, head_shards(): pl.pallas_call(functools.partial(shared_head, span, planes), in_specs=[SM...  8.57 us
    pallas_call x2, Pallas kernels, pack(): pl.pallas_call(pack_body, grid=(count // step,), in_specs=[spec] * 4, out...  5.93 us
    ppermute x6, starting transfers between devices, shift(): return lax.ppermute(block, 'ctx', [(i, i ^ step) for i in range(devices)])  4.96 us
  transfers between devices with their start and end apart: 9, of which 5 were waited for; matrix products, arithmetic and copies ran while one was open for 0% of the time, Pallas kernels for 23%

profile of v1, /device:TPU:1, one launch (start us, length us, event | category | flops | bytes accessed | tf_op | source)
XLA Modules:
  0.0 177.5 jit_solution(8393919050539051410)
XLA Ops:
  0.6 2.0 %pack.3 = bf16[4,512,128]{2,1,0:T(8,128)(2,1)} custom-call(bf16[128,2560]{1,0:T(8,128)(2,1)} %q_ref.3, bf16[128,2560]{1,0:T(8,128)(2,1)} %k_ref.3, bf16[128,2560]{1,0:T(8,128)(2,1)} %v_ref.3, bf16[128,2560]{1,0:T(8,128)(2,1)} %g_ref.3), custom_call_target="tpu_custom_call" | custom-call | tf_op jit(solution)/shard_map/pack/pallas_call | solution.py:221
  2.6 5.4 %all-to-all-start.2 = ((bf16[4,512,128]{2,1,0:T(8,128)(2,1)}), bf16[4,512,128]{2,1,0:T(8,128)(2,1)S(1)}, u32[]{:S(2)}, u32[]{:S(2)}) async-start(bf16[4,512,128]{2,1,0:T(8,128)(2,1)} %pack.3), calls=%async_computation.2 | async-start | bytes 1048576 | tf_op jit(solution)/shard_map/all_to_all | solution.py:498
  8.0 3.9 %pack.2 = bf16[16,512,128]{2,1,0:T(8,128)(2,1)} custom-call(bf16[128,2560]{1,0:T(8,128)(2,1)} %q_ref.3, bf16[128,2560]{1,0:T(8,128)(2,1)} %k_ref.3, bf16[128,2560]{1,0:T(8,128)(2,1)} %v_ref.3, bf16[128,2560]{1,0:T(8,128)(2,1)} %g_ref.3), custom_call_target="tpu_custom_call" | custom-call | tf_op jit(solution)/shard_map/pack/pallas_call | solution.py:221
  12.0 0.0 copy-start
  12.0 10.1 %all-to-all-done.2.own_ref = bf16[4,512,128]{2,1,0:T(8,128)(2,1)S(1)} async-done(((bf16[4,512,128]{2,1,0:T(8,128)(2,1)}), bf16[4,512,128]{2,1,0:T(8,128)(2,1)S(1)}, u32[]{:S(2)}, u32[]{:S(2)}) %all-to-all-start.2) | async-done | bytes 524320 | tf_op jit(solution)/shard_map/all_to_all | solution.py:498
  22.1 5.1 %all-to-all-start = ((bf16[16,512,128]{2,1,0:T(8,128)(2,1)}), bf16[16,512,128]{2,1,0:T(8,128)(2,1)S(1)}, u32[]{:S(2)}, u32[]{:S(2)}) async-start(bf16[16,512,128]{2,1,0:T(8,128)(2,1)} %pack.2), calls=%async_computation | async-start | bytes 4194304 | tf_op jit(solution)/shard_map/all_to_all | solution.py:498
  27.1 0.7 slice.4
  27.9 1.6 collective-permute-start.2
  29.5 0.0 collective-permute-start.1
  29.5 0.5 collective-permute-start
  30.0 0.0 copy-done
  30.0 0.1 copy.11.sel_ref
  30.1 22.4 %collective-permute-done.2.refs_2_ = bf16[4,256,128]{2,1,0:T(8,128)(2,1)S(1)} collective-permute-done((bf16[4,256,128]{2,1,0:T(8,128)(2,1)}, bf16[4,256,128]{2,1,0:T(8,128)(2,1)S(1)}, u32[]{:S(2)}, u32[]{:S(2)}) %collective-permute-start.2) | collective-permute-done | bytes 262176 | tf_op jit(solution)/shard_map/ppermute | solution.py:495
  52.4 6.2 %collective-permute-done.1.refs_1_ = bf16[4,256,128]{2,1,0:T(8,128)(2,1)S(1)} collective-permute-done((bf16[4,256,128]{2,1,0:T(8,128)(2,1)}, bf16[4,256,128]{2,1,0:T(8,128)(2,1)S(1)}, u32[]{:S(2)}, u32[]{:S(2)}) %collective-permute-start.1) | collective-permute-done | bytes 262176 | tf_op jit(solution)/shard_map/ppermute | solution.py:495
  58.6 0.0 collective-permute-done.refs_0_
  58.6 8.6 %shared_head.1 = (bf16[4,256,128]{2,1,0:T(8,128)(2,1)S(1)}, f32[4,264,128]{2,1,0:T(8,128)S(1)}, bf16[4,272,128]{2,1,0:T(8,128)(2,1)S(1)}, bf16[4,272,128]{2,1,0:T(8,128)(2,1)S(1)}, bf16[4,272,128]{2,1,0:T(8,128)(2,1)S(1)}) custom-call(s32[1]{0:T(128)} %bitcast.place_ref, s32[16,8]{1,0:T(8,128)S(1)} %copy.11.sel_ref, ...), custom_call_target="tpu_custom_call" | custom-call | tf_op jit(solution)/shard_map/shared_head/pallas_call | solution.py:506
  67.2 0.7 collective-permute-start.3
  67.9 2.1 %collective-permute-start.4 = (bf16[4,272,128]{2,1,0:T(8,128)(2,1)S(1)}, bf16[4,272,128]{2,1,0:T(8,128)(2,1)S(1)}, u32[]{:S(2)}, u32[]{:S(2)}) collective-permute-start(bf16[4,272,128]{2,1,0:T(8,128)(2,1)S(1)} %get-tuple-element.14), channel_id=1, source_target_pairs={{0,2},{1,3},{2,0},{3,1},{4,6},{5,7},{6,4},{7,5},{8,10},{9,11},{10,... | collective-permute-start | bytes 835592 | tf_op jit(solution)/shard_map/ppermute | solution.py:495
  70.0 0.0 collective-permute-start.5
  70.0 0.0 collective-permute-done.3.refs_0_
  70.1 6.9 %collective-permute-done.4.refs_1_ = bf16[4,272,128]{2,1,0:T(8,128)(2,1)S(1)} collective-permute-done((bf16[4,272,128]{2,1,0:T(8,128)(2,1)S(1)}, bf16[4,272,128]{2,1,0:T(8,128)(2,1)S(1)}, u32[]{:S(2)}, u32[]{:S(2)}) %collective-permute-start.4) | collective-permute-done | bytes 278560 | tf_op jit(solution)/shard_map/ppermute | solution.py:495
  77.0 6.0 %collective-permute-done.5.refs_2_ = bf16[4,272,128]{2,1,0:T(8,128)(2,1)S(1)} collective-permute-done((bf16[4,272,128]{2,1,0:T(8,128)(2,1)S(1)}, bf16[4,272,128]{2,1,0:T(8,128)(2,1)S(1)}, u32[]{:S(2)}, u32[]{:S(2)}) %collective-permute-start.5) | collective-permute-done | bytes 278560 | tf_op jit(solution)/shard_map/ppermute | solution.py:495
  82.9 1.0 gather_terms.1
  83.9 0.0 all-to-all-done.in_ref
  83.9 6.0 %all-to-all-start.3 = ((bf16[4,528,128]{2,1,0:T(8,128)(2,1)}), bf16[4,528,128]{2,1,0:T(8,128)(2,1)S(1)}, u32[]{:S(2)}, u32[]{:S(2)}) async-start(bf16[4,528,128]{2,1,0:T(8,128)(2,1)} %gather_terms.1), calls=%async_computation.3 | async-start | bytes 1081344 | tf_op jit(solution)/shard_map/all_to_all | solution.py:498
  90.0 27.2 %whole_head.1 = bf16[16,528,128]{2,1,0:T(8,128)(2,1)} custom-call(s32[16,8]{1,0:T(8,128)S(1)} %copy.11.sel_ref, bf16[16,512,128]{2,1,0:T(8,128)(2,1)S(1)} %all-to-all-done.in_ref), custom_call_target="tpu_custom_call" | custom-call | tf_op jit(solution)/shard_map/whole_head/pallas_call | solution.py:530
  117.2 0.0 all-to-all-done.3.rest_ref
  117.2 58.3 %all_to_all.20.main_ref = bf16[16,528,128]{2,1,0:T(8,128)(2,1)S(1)} all-to-all(bf16[16,528,128]{2,1,0:T(8,128)(2,1)} %whole_head.1), channel_id=1, replica_groups=mesh['groups'=2,'ctx'=16] {'ctx'}, dimensions={0} | all-to-all | bytes 4325376 | tf_op jit(solution)/shard_map/all_to_all | solution.py:498
  175.5 1.9 %unpack.1 = (bf16[128,2560]{1,0:T(8,128)(2,1)}, bf16[128,2560]{1,0:T(8,128)(2,1)}, bf16[128,2560]{1,0:T(8,128)(2,1)}, bf16[128,2560]{1,0:T(8,128)(2,1)}, f32[2,2560]{1,0:T(2,128)}, /*index=5*/f32[2,2560]{1,0:T(2,128)}) custom-call(bf16[16,528,128]{2,1,0:T(8,128)(2,1)S(1)} %all_to_all.20.main_ref, bf16[4,528,128]{2,1,0:T(8,128)(2,1)S(1)} %all-to-all-done.3.rest_ref), custom_call_target="tpu_custom_call" | custom-call | tf_op jit(solution)/shard_map/unpack/pallas_call | solution.py:542
Async XLA Ops:
  2.6 19.5 %all-to-all-start.2 = ((bf16[4,512,128]{2,1,0:T(8,128)(2,1)}), bf16[4,512,128]{2,1,0:T(8,128)(2,1)S(1)}, u32[]{:S(2)}, u32[]{:S(2)}) async-start(bf16[4,512,128]{2,1,0:T(8,128)(2,1)} %pack.3), calls=%async_computation.2 | async-start | bytes 1048576 | tf_op jit(solution)/shard_map/all_to_all | solution.py:498
  12.0 18.0 %copy-start = (s32[16,8]{0,1:T(8,128)S(1)}, s32[16,8]{0,1:T(8,128)}, u32[]{:S(2)}) copy-start(s32[16,8]{0,1:T(8,128)} %param.9) | copy-start | bytes 1540
  22.1 61.8 %all-to-all-start = ((bf16[16,512,128]{2,1,0:T(8,128)(2,1)}), bf16[16,512,128]{2,1,0:T(8,128)(2,1)S(1)}, u32[]{:S(2)}, u32[]{:S(2)}) async-start(bf16[16,512,128]{2,1,0:T(8,128)(2,1)} %pack.2), calls=%async_computation | async-start | bytes 4194304 | tf_op jit(solution)/shard_map/all_to_all | solution.py:498
  27.9 24.6 %collective-permute-start.2 = (bf16[4,256,128]{2,1,0:T(8,128)(2,1)}, bf16[4,256,128]{2,1,0:T(8,128)(2,1)S(1)}, u32[]{:S(2)}, u32[]{:S(2)}) collective-permute-start(bf16[4,256,128]{2,1,0:T(8,128)(2,1)} %slice.4), channel_id=1, source_target_pairs={{0,3},{1,2},{2,1},{3,0},{4,7},{5,6},{6,5},{7,4},{8,11},{9,10},{10,... | collective-permute-start | bytes 786440 | tf_op jit(solution)/shard_map/ppermute | solution.py:495
  29.5 29.1 %collective-permute-start.1 = (bf16[4,256,128]{2,1,0:T(8,128)(2,1)}, bf16[4,256,128]{2,1,0:T(8,128)(2,1)S(1)}, u32[]{:S(2)}, u32[]{:S(2)}) collective-permute-start(bf16[4,256,128]{2,1,0:T(8,128)(2,1)} %slice.4), channel_id=1, source_target_pairs={{0,2},{1,3},{2,0},{3,1},{4,6},{5,7},{6,4},{7,5},{8,10},{9,11},{10,... | collective-permute-start | bytes 786440 | tf_op jit(solution)/shard_map/ppermute | solution.py:495
  29.5 29.1 %collective-permute-start = (bf16[4,256,128]{2,1,0:T(8,128)(2,1)}, bf16[4,256,128]{2,1,0:T(8,128)(2,1)S(1)}, u32[]{:S(2)}, u32[]{:S(2)}) collective-permute-start(bf16[4,256,128]{2,1,0:T(8,128)(2,1)} %slice.4), channel_id=1, source_target_pairs={{0,1},{1,0},{2,3},{3,2},{4,5},{5,4},{6,7},{7,6},{8,9},{9,8},{10,11... | collective-permute-start | bytes 786440 | tf_op jit(solution)/shard_map/ppermute | solution.py:495
  67.2 2.8 %collective-permute-start.3 = (bf16[4,272,128]{2,1,0:T(8,128)(2,1)S(1)}, bf16[4,272,128]{2,1,0:T(8,128)(2,1)S(1)}, u32[]{:S(2)}, u32[]{:S(2)}) collective-permute-start(bf16[4,272,128]{2,1,0:T(8,128)(2,1)S(1)} %get-tuple-element.13), channel_id=1, source_target_pairs={{0,1},{1,0},{2,3},{3,2},{4,5},{5,4},{6,7},{7,6},{8,9},{9,8},{10,11... | collective-permute-start | bytes 835592 | tf_op jit(solution)/shard_map/ppermute | solution.py:495
  67.9 9.0 %collective-permute-start.4 = (bf16[4,272,128]{2,1,0:T(8,128)(2,1)S(1)}, bf16[4,272,128]{2,1,0:T(8,128)(2,1)S(1)}, u32[]{:S(2)}, u32[]{:S(2)}) collective-permute-start(bf16[4,272,128]{2,1,0:T(8,128)(2,1)S(1)} %get-tuple-element.14), channel_id=1, source_target_pairs={{0,2},{1,3},{2,0},{3,1},{4,6},{5,7},{6,4},{7,5},{8,10},{9,11},{10,... | collective-permute-start | bytes 835592 | tf_op jit(solution)/shard_map/ppermute | solution.py:495
  70.0 12.9 %collective-permute-start.5 = (bf16[4,272,128]{2,1,0:T(8,128)(2,1)S(1)}, bf16[4,272,128]{2,1,0:T(8,128)(2,1)S(1)}, u32[]{:S(2)}, u32[]{:S(2)}) collective-permute-start(bf16[4,272,128]{2,1,0:T(8,128)(2,1)S(1)} %get-tuple-element.15), channel_id=1, source_target_pairs={{0,3},{1,2},{2,1},{3,0},{4,7},{5,6},{6,5},{7,4},{8,11},{9,10},{10,... | collective-permute-start | bytes 835592 | tf_op jit(solution)/shard_map/ppermute | solution.py:495
  83.9 33.3 %all-to-all-start.3 = ((bf16[4,528,128]{2,1,0:T(8,128)(2,1)}), bf16[4,528,128]{2,1,0:T(8,128)(2,1)S(1)}, u32[]{:S(2)}, u32[]{:S(2)}) async-start(bf16[4,528,128]{2,1,0:T(8,128)(2,1)} %gather_terms.1), calls=%async_computation.3 | async-start | bytes 1081344 | tf_op jit(solution)/shard_map/all_to_all | solution.py:498

commit v2 on v0

--- a/solution.py
+++ b/solution.py
@@ -1,7 +1,12 @@
+import functools
+
 import jax
 import jax.numpy as jnp
 from jax import lax
+from jax.experimental import pallas as pl
+from jax.experimental.pallas import tpu as pltpu
 from jax.sharding import PartitionSpec as P
+
 
 HEADS = 20
 HEAD_DIM = 128
@@ -73,7 +78,7 @@
     )
 
 
-def shards(query_rows, key_rows, value_rows, out_grad, selected):
+def listed_shards(query_rows, key_rows, value_rows, out_grad, selected):
     height, columns = query_rows.shape
     devices = lax.axis_size("ctx")
     tiles_here = height // TILE
@@ -159,6 +164,424 @@
     return (attended, grad_query, grad_key, grad_value, own_coarse_keys, own_coarse_values)
 
 
+LANES = 128
+JOBS = 4
+SPLITS = 3
+VMEM = pl.BlockSpec(memory_space=pltpu.VMEM)
+SMEM = pl.BlockSpec(memory_space=pltpu.SMEM)
+BIG = pltpu.CompilerParams(vmem_limit_bytes=50 * 1024 * 1024)
+
+
+def nt(left, right):
+    return contract(left, right, 1, 1)
+
+
+def nn(left, right):
+    return contract(left, right, 1, 0)
+
+
+def split_rows(total):
+    parts = []
+    for _ in range(SPLITS):
+        part = total.astype(jnp.bfloat16)
+        parts.append(part.astype(jnp.float32))
+        total = total - parts[-1]
+    return parts
+
+
+def tail_rows(coarse_key, coarse_value):
+    per_tile = TILE // POOL
+    parts = split_rows(jnp.concatenate([coarse_key, coarse_value], axis=0))
+    used = SPLITS * 2 * per_tile
+    filler = jnp.zeros((tail_height() - used, LANES), jnp.float32)
+    return jnp.concatenate(parts + [filler], axis=0).astype(jnp.bfloat16)
+
+
+def tail_height():
+    used = SPLITS * 2 * (TILE // POOL)
+    return -(-used // 16) * 16
+
+
+def join_tail(tail):
+    pair = 2 * (TILE // POOL)
+    rows = tail.astype(jnp.float32)
+    total = rows[:pair]
+    for part in range(1, SPLITS):
+        total = total + rows[part * pair : (part + 1) * pair]
+    return total
+
+
+def lane_block(index):
+    return pl.ds(pl.multiple_of(index * LANES, LANES), LANES)
+
+
+def pack_body(heads, span, place_ref, q_ref, k_ref, v_ref, g_ref, *out_refs):
+    place = place_ref[0]
+    for step, out_ref in enumerate(out_refs):
+        if step < heads:
+            head = lax.bitwise_xor(place, step)
+        else:
+            head = heads + lax.bitwise_xor(place // span, step - heads)
+        for index, ref in enumerate((q_ref, k_ref, v_ref, g_ref)):
+            out_ref[index * TILE : (index + 1) * TILE, :] = ref[:, lane_block(head)]
+
+
+def pack(arrays, place, devices, span):
+    return pl.pallas_call(
+        functools.partial(pack_body, devices, span),
+        in_specs=[SMEM] + [VMEM] * 4,
+        out_specs=[VMEM] * HEADS,
+        out_shape=[jax.ShapeDtypeStruct((4 * TILE, LANES), jnp.bfloat16)] * HEADS,
+        compiler_params=BIG,
+        cost_estimate=pl.CostEstimate(
+            flops=0, transcendentals=0, bytes_accessed=16 * HEADS * TILE * LANES
+        ),
+        name="pack",
+    )(place, *arrays)
+
+
+def prepare(scratch):
+    rows_ref, pool_key, pool_value, key_t, value_t, both_sum, pool_key_sum, pool_value_sum = scratch
+    per_tile = TILE // POOL
+
+    def one(tile, carry):
+        for place, pool_ref, flip_ref in ((0, pool_key, key_t), (1, pool_value, value_t)):
+            rows = rows_ref[tile, :, place * LANES : (place + 1) * LANES].astype(jnp.float32)
+            means = [
+                jnp.mean(rows[part * POOL : (part + 1) * POOL], axis=0, keepdims=True)
+                for part in range(per_tile)
+            ]
+            pool_ref[pl.ds(tile * per_tile, per_tile), :] = jnp.concatenate(means, axis=0)
+            flip_ref[tile] = rows.T.astype(jnp.bfloat16)
+        both_sum[tile] = jnp.zeros((TILE, 2 * LANES), jnp.float32)
+        return carry
+
+    lax.fori_loop(0, rows_ref.shape[0], one, 0)
+    pool_key_sum[...] = jnp.zeros_like(pool_key_sum)
+    pool_value_sum[...] = jnp.zeros_like(pool_value_sum)
+
+
+def wide_pair(left, right):
+    zeros = jnp.zeros_like(left)
+    return jnp.concatenate(
+        [jnp.concatenate([left, zeros], axis=1), jnp.concatenate([zeros, right], axis=1)], axis=0
+    )
+
+
+def some_tiles(jobs, scratch, work):
+    rows_ref, pool_key, pool_value, key_t, value_t, both_sum, pool_key_sum, pool_value_sum = scratch
+    scaling = HEAD_DIM ** (-0.5)
+    base2 = scaling * 1.4426950408889634
+    comp = pool_key.shape[0]
+    coarse_key = pool_key[...].astype(jnp.bfloat16)
+    coarse_value = pool_value[...].astype(jnp.bfloat16)
+    coarse = jnp.concatenate([coarse_key, coarse_value], axis=1)
+    fine = SEL * TILE
+    spans = [(slot * TILE, TILE) for slot in range(SEL)] + [(fine, comp)]
+    results = []
+    for (query, grad, listed), (score_ref, prob_ref, pair_ref) in zip(jobs, work):
+        pair = wide_pair(query, grad)
+        rows = [rows_ref[tile] for tile in listed]
+        both = nt(jnp.concatenate(rows + [coarse], axis=0), pair)
+        score_ref[...] = both[:, :LANES]
+        prob_ref[...] = both[:, LANES:]
+        top = jnp.max(both[:, :LANES], axis=0, keepdims=True)
+        results.append((pair, top))
+    for index, (_, (score_ref, prob_ref, pair_ref)) in enumerate(zip(jobs, work)):
+        pair, top = results[index]
+        raised = jnp.exp2((score_ref[...] - top) * base2)
+        score_ref[...] = raised
+        inverse = 1.0 / jnp.sum(raised, axis=0, keepdims=True)
+        results[index] = (pair, inverse)
+    outs = []
+    for index, ((query, grad, listed), (score_ref, prob_ref, pair_ref)) in enumerate(zip(jobs, work)):
+        pair, inverse = results[index]
+        weight = score_ref[...] * inverse
+        rounded = weight.astype(jnp.bfloat16)
+        pair_ref[:, LANES:] = rounded
+        score_ref[...] = weight
+        values_t = jnp.concatenate([value_t[tile] for tile in listed], axis=1)
+        out_t = nn(values_t, pair_ref[:fine, LANES:]) + contract(
+            coarse_value, pair_ref[fine:, LANES:], 0, 0
+        )
+        out_t = out_t.astype(jnp.bfloat16).astype(jnp.float32)
+        dots = jnp.sum(out_t * grad.astype(jnp.float32).T, axis=0, keepdims=True)
+        outs.append((out_t, dots))
+    for index, ((query, grad, listed), (score_ref, prob_ref, pair_ref)) in enumerate(zip(jobs, work)):
+        out_t, dots = outs[index]
+        slope = (score_ref[...] * (prob_ref[...] - dots)).astype(jnp.bfloat16)
+        pair_ref[:, :LANES] = slope
+        terms = nn(pair_ref[...], results[index][0])
+        for tile, (start, size) in zip(listed, spans):
+            both_sum[tile] += terms[start : start + size]
+        pool_key_sum[...] += terms[fine:, :LANES]
+        pool_value_sum[...] += terms[fine:, LANES:]
+        keys_t = jnp.concatenate([key_t[tile] for tile in listed], axis=1)
+        query_t = nn(keys_t, pair_ref[:fine, :LANES]) + contract(
+            coarse_key, pair_ref[fine:, :LANES], 0, 0
+        )
+        outs[index] = (
+            out_t.T.astype(jnp.bfloat16),
+            (query_t.T * scaling).astype(jnp.bfloat16),
+        )
+    return outs
+
+
+def finish(tile, scratch):
+    scaling = HEAD_DIM ** (-0.5)
+    both_sum, pool_key_sum, pool_value_sum = scratch
+    per_tile = TILE // POOL
+    coarse_key = pool_key_sum[pl.ds(tile * per_tile, per_tile), :] * scaling
+    coarse_value = pool_value_sum[pl.ds(tile * per_tile, per_tile), :]
+
+    def whole(fine, coarse):
+        return jnp.concatenate(
+            [
+                fine[part * POOL : (part + 1) * POOL] + coarse[part : part + 1] * (1.0 / POOL)
+                for part in range(per_tile)
+            ],
+            axis=0,
+        )
+
+    return (
+        whole(both_sum[tile, :, :LANES] * scaling, coarse_key),
+        whole(both_sum[tile, :, LANES:], coarse_value),
+        coarse_key,
+        coarse_value,
+    )
+
+
+def head_scratch(tiles):
+    comp = tiles * (TILE // POOL)
+    keys = SEL * TILE + comp
+    return [
+        pltpu.VMEM((tiles, TILE, 2 * LANES), jnp.bfloat16),
+        pltpu.VMEM((comp, LANES), jnp.float32),
+        pltpu.VMEM((comp, LANES), jnp.float32),
+        pltpu.VMEM((tiles, LANES, TILE), jnp.bfloat16),
+        pltpu.VMEM((tiles, LANES, TILE), jnp.bfloat16),
+        pltpu.VMEM((tiles, TILE, 2 * LANES), jnp.float32),
+        pltpu.VMEM((comp, LANES), jnp.float32),
+        pltpu.VMEM((comp, LANES), jnp.float32),
+    ] + JOBS * [
+        pltpu.VMEM((keys, LANES), jnp.float32),
+        pltpu.VMEM((keys, LANES), jnp.float32),
+        pltpu.VMEM((keys, 2 * LANES), jnp.bfloat16),
+    ]
+
+
+def split_scratch(scratch):
+    totals, work = scratch[:8], scratch[8:]
+    return totals, [work[3 * job : 3 * job + 3] for job in range(JOBS)]
+
+
+def head_cost(queries, keys, moved):
+    return pl.CostEstimate(
+        flops=12 * queries * keys * LANES,
+        transcendentals=queries * keys,
+        bytes_accessed=moved,
+    )
+
+
+def every_tile(count, stride, place_ref, sel_ref, query_ref, out_ref, totals, work):
+    place = place_ref[0]
+
+    def some(first, carry):
+        jobs = []
+        for job in range(JOBS):
+            piece = first * JOBS + job
+            tile = lax.bitwise_xor(place, piece * stride)
+            listed = [lax.bitwise_xor(sel_ref[tile, slot], place) for slot in range(SEL)]
+            jobs.append((query_ref[piece, :, :LANES], query_ref[piece, :, LANES:], listed))
+        for job, (rows, slopes) in enumerate(some_tiles(jobs, totals, work)):
+            out_ref[first * JOBS + job, :TILE, :] = rows
+            out_ref[first * JOBS + job, TILE : 2 * TILE, :] = slopes
+        return carry
+
+    lax.fori_loop(0, count // JOBS, some, 0)
+
+
+def whole_head(tiles, place_ref, sel_ref, *refs):
+    pieces, outs = refs[:tiles][::-1], refs[tiles : 2 * tiles]
+    query_ref, out_ref = refs[2 * tiles : 2 * tiles + 2]
+    totals, work = split_scratch(refs[2 * tiles + 2 :])
+    for step, piece in enumerate(pieces):
+        query_ref[step, :, :LANES] = piece[:TILE, :]
+        totals[0][step, :, :LANES] = piece[TILE : 2 * TILE, :]
+        totals[0][step, :, LANES:] = piece[2 * TILE : 3 * TILE, :]
+        query_ref[step, :, LANES:] = piece[3 * TILE :, :]
+    prepare(totals)
+    every_tile(tiles, 1, place_ref, sel_ref, query_ref, out_ref, totals, work)
+    for step, out in enumerate(outs):
+        key, value, coarse_key, coarse_value = finish(step, totals[5:])
+        out[: 2 * TILE, :] = out_ref[step]
+        out[2 * TILE : 3 * TILE, :] = key.astype(jnp.bfloat16)
+        out[3 * TILE : 4 * TILE, :] = value.astype(jnp.bfloat16)
+        out[4 * TILE :, :] = tail_rows(coarse_key, coarse_value)
+
+
+def shared_head(span, planes, place_ref, sel_ref, *refs):
+    owns, refs = refs[:planes], refs[planes:]
+    pieces, refs = refs[: span - 1], refs[span - 1 :]
+    out_ref, keep_ref = refs[:2]
+    send_refs = refs[2 : span + 1]
+    query_ref = refs[span + 1]
+    totals, work = split_scratch(refs[span + 2 :])
+    for plane, own in enumerate(owns):
+        query_ref[plane, :, :LANES] = own[:TILE, :]
+        query_ref[plane, :, LANES:] = own[3 * TILE :, :]
+        totals[0][plane * span, :, :LANES] = own[TILE : 2 * TILE, :]
+        totals[0][plane * span, :, LANES:] = own[2 * TILE : 3 * TILE, :]
+        for step in range(1, span):
+            piece = pieces[step - 1]
+            totals[0][plane * span + step, :, :LANES] = piece[plane, :TILE, :]
+            totals[0][plane * span + step, :, LANES:] = piece[plane, TILE:, :]
+    prepare(totals)
+    every_tile(planes, span, place_ref, sel_ref, query_ref, out_ref, totals, work)
+    for step in range(span):
+
+        def last(plane, carry, step=step):
+            key, value, coarse_key, coarse_value = finish(plane * span + step, totals[5:])
+            if step == 0:
+                pair = 2 * (TILE // POOL)
+                keep_ref[plane, :TILE, :] = key
+                keep_ref[plane, TILE : 2 * TILE, :] = value
+                keep_ref[plane, 2 * TILE : 2 * TILE + 8, :] = jnp.concatenate(
+                    [coarse_key, coarse_value, jnp.zeros((8 - pair, LANES), jnp.float32)], axis=0
+                )
+            else:
+                ref = send_refs[step - 1]
+                ref[plane, :TILE, :] = key.astype(jnp.bfloat16)
+                ref[plane, TILE : 2 * TILE, :] = value.astype(jnp.bfloat16)
+                ref[plane, 2 * TILE :, :] = tail_rows(coarse_key, coarse_value)
+            return carry
+
+        lax.fori_loop(0, planes, last, 0)
+
+
+def gather_terms(span, rows_ref, keep_ref, *refs):
+    pieces, outs = refs[: span - 1], refs[span - 1 :]
+    per_tile = TILE // POOL
+    for plane, out in enumerate(outs):
+        fine = keep_ref[plane, : 2 * TILE, :]
+        coarse = keep_ref[plane, 2 * TILE : 2 * TILE + 2 * per_tile, :]
+        for piece in pieces:
+            fine = fine + piece[plane, : 2 * TILE, :].astype(jnp.float32)
+            coarse = coarse + join_tail(piece[plane, 2 * TILE :, :])
+        out[: 2 * TILE, :] = rows_ref[plane]
+        out[2 * TILE : 4 * TILE, :] = fine.astype(jnp.bfloat16)
+        out[4 * TILE :, :] = tail_rows(coarse[:per_tile], coarse[per_tile:])
+
+
+def unpack_body(heads, span, place_ref, *refs):
+    pieces, (a_ref, q_ref, k_ref, v_ref, pk_ref, pv_ref) = refs[:-6], refs[-6:]
+    pieces = pieces[:heads][::-1] + pieces[heads:][::-1]
+    per_tile = TILE // POOL
+    place = place_ref[0]
+    for step, ref in enumerate(pieces):
+        if step < heads:
+            head = lax.bitwise_xor(place, step)
+        else:
+            head = heads + lax.bitwise_xor(place // span, step - heads)
+        columns = lane_block(head)
+        for index, out in enumerate((a_ref, q_ref, k_ref, v_ref)):
+            out[:, columns] = ref[index * TILE : (index + 1) * TILE, :]
+        coarse = join_tail(ref[4 * TILE :, :])
+        pk_ref[:, columns] = coarse[:per_tile]
+        pv_ref[:, columns] = coarse[per_tile:]
+
+
+def head_shards(query_rows, key_rows, value_rows, out_grad, selected):
+    devices = lax.axis_size("ctx")
+    height, columns = query_rows.shape
+    planes = HEADS - devices
+    span = devices // planes
+    arrays = (query_rows, key_rows, value_rows, out_grad)
+    place = jnp.reshape(lax.axis_index("ctx"), (1,))
+
+    def shift(block, step):
+        return lax.ppermute(block, "ctx", [(i, i ^ step) for i in range(devices)])
+
+    def spread(pieces, stride):
+        moved = [pieces[0]]
+        for step in range(1, len(pieces)):
+            moved.append(shift(pieces[step], step * stride))
+        return moved
+
+    def shape(*dims, dtype=jnp.bfloat16):
+        return jax.ShapeDtypeStruct(dims, dtype)
+
+    block = 4 * TILE + tail_height()
+    part = 2 * TILE + tail_height()
+    keys = SEL * TILE + devices * (TILE // POOL)
+    packed = pack(arrays, place, devices, span)
+    owns = spread(packed[devices:], span)
+    mains = spread(packed[:devices], 1)
+    own_kv = jnp.stack([own[TILE : 3 * TILE] for own in owns])
+    pieces = [shift(own_kv, step) for step in range(1, span)]
+    outs = pl.pallas_call(
+        functools.partial(shared_head, span, planes),
+        in_specs=[SMEM, SMEM] + [VMEM] * (planes + span - 1),
+        out_specs=[VMEM] * (span + 1),
+        out_shape=[
+            shape(planes, 2 * TILE, LANES),
+            shape(planes, 2 * TILE + 8, LANES, dtype=jnp.float32),
+        ]
+        + [shape(planes, part, LANES)] * (span - 1),
+        scratch_shapes=[pltpu.VMEM((planes, TILE, 2 * LANES), jnp.bfloat16)]
+        + head_scratch(devices),
+        compiler_params=BIG,
+        cost_estimate=head_cost(planes * TILE, keys, 16 * devices * TILE * LANES),
+        name="shared_head",
+    )(place, selected, *owns, *pieces)
+    terms = [shift(sent, step + 1) for step, sent in enumerate(outs[2:])]
+    rests = pl.pallas_call(
+        functools.partial(gather_terms, span),
+        in_specs=[VMEM] * (span + 1),
+        out_specs=[VMEM] * planes,
+        out_shape=[shape(block, LANES)] * planes,
+        compiler_params=BIG,
+        name="gather_terms",
+    )(outs[0], outs[1], *terms)
+    rests = spread(rests, span)
+    dones = pl.pallas_call(
+        functools.partial(whole_head, devices),
+        in_specs=[SMEM, SMEM] + [VMEM] * devices,
+        out_specs=[VMEM] * devices,
+        out_shape=[shape(block, LANES)] * devices,
+        scratch_shapes=[
+            pltpu.VMEM((devices, TILE, 2 * LANES), jnp.bfloat16),
+            pltpu.VMEM((devices, 2 * TILE, LANES), jnp.bfloat16),
+        ]
+        + head_scratch(devices),
+        compiler_params=BIG,
+        cost_estimate=head_cost(devices * TILE, keys, 16 * devices * TILE * LANES),
+        name="whole_head",
+    )(place, selected, *mains[::-1])
+    dones = spread(dones, 1)
+    wide = shape(height, columns)
+    thin = shape(height // POOL, columns, dtype=jnp.float32)
+    return pl.pallas_call(
+        functools.partial(unpack_body, devices, span),
+        in_specs=[SMEM] + [VMEM] * HEADS,
+        out_specs=[VMEM] * 6,
+        out_shape=[wide, wide, wide, wide, thin, thin],
+        compiler_params=BIG,
+        name="unpack",
+    )(place, *dones[::-1], *rests[::-1])
+
+
+def shards(query_rows, key_rows, value_rows, out_grad, selected):
+    devices = lax.axis_size("ctx")
+    planes = HEADS - devices
+    tiles_here = query_rows.shape[0] // TILE
+    if planes > 0 and devices % planes == 0 and tiles_here == 1 and planes % JOBS == 0:
+        span = devices // planes
+        if span & (span - 1) == 0:
+            return head_shards(query_rows, key_rows, value_rows, out_grad, selected)
+    return listed_shards(query_rows, key_rows, value_rows, out_grad, selected)
+
+
 def solution(mesh):
     in_specs = (
         P(("groups", "ctx"), None),
@@ -175,4 +598,6 @@
         P(("groups", "ctx"), None),
         P(("groups", "ctx"), None),
     )
-    return jax.shard_map(shards, mesh=mesh, in_specs=in_specs, out_specs=out_specs, check_vma=False)
+    return jax.shard_map(
+        shards, mesh=mesh, in_specs=in_specs, out_specs=out_specs, check_vma=False
+    )

time: 682 us -> 168 us (0.25); the launches traced: 675 us -> 168 us
  waiting for transfers between devices: 311 us -> 58.9 us
  matrix products: 105 us -> 0 us
  local copies, waits for them, and re-layouts: 92.8 us -> 2.27 us
  starting transfers between devices: 119 us -> 79.4 us
  other arithmetic: 29.9 us -> 0.04 us
  Pallas kernels: 0 us -> 26.6 us
  between operations: 16.6 us -> 0.74 us
    all_to_all x8 -> x0, waiting for transfers between devices: 291 us -> none  [the longest x1 81 us: shards(): lax.all_to_all(listed_keys, 'ctx', split_axis=1, concat_axis=0, tiled=True)]
    all_to_all x8 -> x0, starting transfers between devices: 119 us -> none  [the longest x1 24.1 us: shards(): lax.all_to_all(held_value_grad, 'ctx', split_axis=0, concat_axis=2, tiled...]
    dot_general x122 -> x0, matrix products: 105 us -> none  [the longest x80 62.3 us: contract(): lax.dot_general(left, right, (((left_dim,), (right_dim,)), ((), ())), pre...]
    ppermute x0 -> x42, starting transfers between devices: none -> 79.4 us  [shift(): return lax.ppermute(block, 'ctx', [(i, i ^ step) for i in range(devices)])]
    ppermute x0 -> x42, waiting for transfers between devices: none -> 58.9 us  [shift(): return lax.ppermute(block, 'ctx', [(i, i ^ step) for i in range(devices)])]
    unnamed x360 -> x7, local copies, waits for them, and re-layouts: 43 us -> 2.24 us
    pallas_call x0 -> x5, Pallas kernels: none -> 26.6 us  [the longest x1 16.6 us: head_shards(): pl.pallas_call(functools.partial(whole_head, devices), in_specs=[SMEM, SM...]
    all_to_all x6 -> x0, local copies, waits for them, and re-layouts: 20.6 us -> none  [the longest x2 7.78 us: shards(): lax.all_to_all(package(key_tiles, own_keys, devices, spread), 'ctx', spli...]
  transfers between devices with their start and end apart: 9 -> 42, of which waited for: 8 -> 17; matrix products, arithmetic and copies ran while one was open for 23% -> 0% of each run, Pallas kernels for 0% -> 14%
where the time goes in v2:
time: 168 us
  starting transfers between devices  79.4 us (47%)
  waiting for transfers between devices  58.9 us (35%)
  Pallas kernels  26.6 us (16%)
  local copies, waits for them, and re-layouts  2.27 us (1%)
    ppermute x42, starting transfers between devices, shift(): return lax.ppermute(block, 'ctx', [(i, i ^ step) for i in range(devices)])  79.4 us
    ppermute x42, waiting for transfers between devices, shift(): return lax.ppermute(block, 'ctx', [(i, i ^ step) for i in range(devices)])  58.9 us
    pallas_call x1, Pallas kernels, head_shards(): pl.pallas_call(functools.partial(whole_head, devices), in_specs=[SMEM, SM...  16.6 us
    pallas_call x1, Pallas kernels, head_shards(): pl.pallas_call(functools.partial(shared_head, span, planes), in_specs=[SM...  6.12 us
  transfers between devices with their start and end apart: 42, of which 17 were waited for; matrix products, arithmetic and copies ran while one was open for 0% of the time, Pallas kernels for 14%

profile of v2, /device:TPU:1, one launch (start us, length us, event | category | flops | bytes accessed | tf_op | source)
XLA Modules:
  0.0 168.0 jit_solution(3339843417916187560)
XLA Ops:
  0.6 1.1 copy-done
  1.7 1.1 copy-done.1
  2.8 1.8 %pack.1 = (bf16[512,128]{1,0:T(8,128)(2,1)S(1)}, bf16[512,128]{1,0:T(8,128)(2,1)S(1)}, bf16[512,128]{1,0:T(8,128)(2,1)S(1)}, bf16[512,128]{1,0:T(8,128)(2,1)S(1)...) custom-call(s32[1]{0:T(128)} %bitcast.place_ref, ...), custom_call_target="tpu_custom_call" | custom-call | bytes 5242880 | tf_op jit(solution)/shard_map/pack/pallas_call | solution.py:230
  4.6 5.7 %collective-permute-start = (bf16[512,128]{1,0:T(8,128)(2,1)S(1)}, bf16[512,128]{1,0:T(8,128)(2,1)S(1)}, u32[]{:S(2)}, u32[]{:S(2)}) collective-permute-start(bf16[512,128]{1,0:T(8,128)(2,1)S(1)} %get-tuple-element.51), channel_id=1, source_target_pairs={{0,15},{1,14},{2,13},{3,12},{4,11},{5,10},{6,9},{7,8},{8,7},{9,6},... | collective-permute-start | bytes 393224 | tf_op jit(solution)/shard_map/ppermute | solution.py:503
  10.3 3.2 %collective-permute-start.2 = (bf16[512,128]{1,0:T(8,128)(2,1)S(1)}, bf16[512,128]{1,0:T(8,128)(2,1)S(1)}, u32[]{:S(2)}, u32[]{:S(2)}) collective-permute-start(bf16[512,128]{1,0:T(8,128)(2,1)S(1)} %get-tuple-element.53), channel_id=1, source_target_pairs={{0,13},{1,12},{2,15},{3,14},{4,9},{5,8},{6,11},{7,10},{8,5},{9,4},... | collective-permute-start | bytes 393224 | tf_op jit(solution)/shard_map/ppermute | solution.py:503
  14.0 13.2 %collective-permute-start.4 = (bf16[512,128]{1,0:T(8,128)(2,1)S(1)}, bf16[512,128]{1,0:T(8,128)(2,1)S(1)}, u32[]{:S(2)}, u32[]{:S(2)}) collective-permute-start(bf16[512,128]{1,0:T(8,128)(2,1)S(1)} %get-tuple-element.55), channel_id=1, source_target_pairs={{0,11},{1,10},{2,9},{3,8},{4,15},{5,14},{6,13},{7,12},{8,3},{9,2},... | collective-permute-start | bytes 393224 | tf_op jit(solution)/shard_map/ppermute | solution.py:503
  27.2 2.5 %collective-permute-start.5 = (bf16[512,128]{1,0:T(8,128)(2,1)S(1)}, bf16[512,128]{1,0:T(8,128)(2,1)S(1)}, u32[]{:S(2)}, u32[]{:S(2)}) collective-permute-start(bf16[512,128]{1,0:T(8,128)(2,1)S(1)} %get-tuple-element.56), channel_id=1, source_target_pairs={{0,10},{1,11},{2,8},{3,9},{4,14},{5,15},{6,12},{7,13},{8,2},{9,3},... | collective-permute-start | bytes 393224 | tf_op jit(solution)/shard_map/ppermute | solution.py:503
  29.7 10.6 %collective-permute-start.6 = (bf16[512,128]{1,0:T(8,128)(2,1)S(1)}, bf16[512,128]{1,0:T(8,128)(2,1)S(1)}, u32[]{:S(2)}, u32[]{:S(2)}) collective-permute-start(bf16[512,128]{1,0:T(8,128)(2,1)S(1)} %get-tuple-element.57), channel_id=1, source_target_pairs={{0,9},{1,8},{2,11},{3,10},{4,13},{5,12},{6,15},{7,14},{8,1},{9,0},... | collective-permute-start | bytes 393224 | tf_op jit(solution)/shard_map/ppermute | solution.py:503
  40.3 2.5 %collective-permute-start.7 = (bf16[512,128]{1,0:T(8,128)(2,1)S(1)}, bf16[512,128]{1,0:T(8,128)(2,1)S(1)}, u32[]{:S(2)}, u32[]{:S(2)}) collective-permute-start(bf16[512,128]{1,0:T(8,128)(2,1)S(1)} %get-tuple-element.58), channel_id=1, source_target_pairs={{0,8},{1,9},{2,10},{3,11},{4,12},{5,13},{6,14},{7,15},{8,0},{9,1},... | collective-permute-start | bytes 393224 | tf_op jit(solution)/shard_map/ppermute | solution.py:503
  42.9 7.0 %collective-permute-done.4.refs_4_ = bf16[512,128]{1,0:T(8,128)(2,1)S(1)} collective-permute-done((bf16[512,128]{1,0:T(8,128)(2,1)S(1)}, bf16[512,128]{1,0:T(8,128)(2,1)S(1)}, u32[]{:S(2)}, u32[]{:S(2)}) %collective-permute-start.4) | collective-permute-done | bytes 131104 | tf_op jit(solution)/shard_map/ppermute | solution.py:503
  49.8 2.8 %collective-permute-done.5.refs_5_ = bf16[512,128]{1,0:T(8,128)(2,1)S(1)} collective-permute-done((bf16[512,128]{1,0:T(8,128)(2,1)S(1)}, bf16[512,128]{1,0:T(8,128)(2,1)S(1)}, u32[]{:S(2)}, u32[]{:S(2)}) %collective-permute-start.5) | collective-permute-done | bytes 131104 | tf_op jit(solution)/shard_map/ppermute | solution.py:503
  52.6 3.0 %collective-permute-done.31.refs_2_ = bf16[512,128]{1,0:T(8,128)(2,1)S(1)} collective-permute-done((bf16[512,128]{1,0:T(8,128)(2,1)S(1)}, bf16[512,128]{1,0:T(8,128)(2,1)S(1)}, u32[]{:S(2)}, u32[]{:S(2)}) %collective-permute-start.31) | collective-permute-done | bytes 131104 | tf_op jit(solution)/shard_map/ppermute | solution.py:503
  55.6 2.2 %collective-permute-start.32 = (bf16[512,128]{1,0:T(8,128)(2,1)S(1)}, bf16[512,128]{1,0:T(8,128)(2,1)S(1)}, u32[]{:S(2)}, u32[]{:S(2)}) collective-permute-start(bf16[512,128]{1,0:T(8,128)(2,1)S(1)} %get-tuple-element.86), channel_id=1, source_target_pairs={{0,12},{1,13},{2,14},{3,15},{4,8},{5,9},{6,10},{7,11},{8,4},{9,5},... | collective-permute-start | bytes 393224 | tf_op jit(solution)/shard_map/ppermute | solution.py:503
  57.8 0.7 collective-permute-done.6.refs_6_
  58.5 5.6 %collective-permute-done.7.refs_7_ = bf16[512,128]{1,0:T(8,128)(2,1)S(1)} collective-permute-done((bf16[512,128]{1,0:T(8,128)(2,1)S(1)}, bf16[512,128]{1,0:T(8,128)(2,1)S(1)}, u32[]{:S(2)}, u32[]{:S(2)}) %collective-permute-start.7) | collective-permute-done | bytes 131104 | tf_op jit(solution)/shard_map/ppermute | solution.py:503
  64.1 2.7 %collective-permute-done.8.refs_8_ = bf16[512,128]{1,0:T(8,128)(2,1)S(1)} collective-permute-done((bf16[512,128]{1,0:T(8,128)(2,1)S(1)}, bf16[512,128]{1,0:T(8,128)(2,1)S(1)}, u32[]{:S(2)}, u32[]{:S(2)}) %collective-permute-start.8) | collective-permute-done | bytes 131104 | tf_op jit(solution)/shard_map/ppermute | solution.py:503
  66.8 1.5 collective-permute-start.12
  68.3 1.3 collective-permute-done.9.refs_9_
  69.6 1.2 collective-permute-start.13
  70.8 0.7 collective-permute-start.14
  71.6 0.9 collective-permute-done.10.refs_10_
  73.0 2.3 %collective-permute-done.11.refs_11_ = bf16[512,128]{1,0:T(8,128)(2,1)S(1)} collective-permute-done((bf16[512,128]{1,0:T(8,128)(2,1)S(1)}, bf16[512,128]{1,0:T(8,128)(2,1)S(1)}, u32[]{:S(2)}, u32[]{:S(2)}) %collective-permute-start.11) | collective-permute-done | bytes 131104 | tf_op jit(solution)/shard_map/ppermute | solution.py:503
  75.5 0.7 collective-permute-start.33
  76.2 16.6 %whole_head.1 = (bf16[528,128]{1,0:T(8,128)(2,1)S(1)}, bf16[528,128]{1,0:T(8,128)(2,1)S(1)}, bf16[528,128]{1,0:T(8,128)(2,1)S(1)}, bf16[528,128]{1,0:T(8,128)(2,...) custom-call(s32[1]{0:T(128)} %bitcast.place_ref, ...), custom_call_target="tpu_custom_call" | custom-call | flops 3321888768 | bytes 4194304 | tf_op jit(solution)/shard_map/whole_head/pallas_call | solution.py:547
  92.8 3.2 %collective-permute-start.15 = (bf16[528,128]{1,0:T(8,128)(2,1)}, bf16[528,128]{1,0:T(8,128)(2,1)S(1)}, u32[]{:S(2)}, u32[]{:S(2)}) collective-permute-start(bf16[528,128]{1,0:T(8,128)(2,1)} %get-tuple-element.67), channel_id=1, source_target_pairs={{0,15},{1,14},{2,13},{3,12},{4,11},{5,10},{6,9},{7,8},{8,7},{9,6},... | collective-permute-start | bytes 405512 | tf_op jit(solution)/shard_map/ppermute | solution.py:503
  96.0 0.9 collective-permute-start.16
  96.9 2.8 %collective-permute-start.17 = (bf16[528,128]{1,0:T(8,128)(2,1)S(1)}, bf16[528,128]{1,0:T(8,128)(2,1)S(1)}, u32[]{:S(2)}, u32[]{:S(2)}) collective-permute-start(bf16[528,128]{1,0:T(8,128)(2,1)S(1)} %get-tuple-element.69), channel_id=1, source_target_pairs={{0,13},{1,12},{2,15},{3,14},{4,9},{5,8},{6,11},{7,10},{8,5},{9,4},... | collective-permute-start | bytes 405512 | tf_op jit(solution)/shard_map/ppermute | solution.py:503
  99.7 1.1 collective-permute-start.18
  100.8 6.1 %shared_head.1 = (bf16[4,256,128]{2,1,0:T(8,128)(2,1)S(1)}, f32[4,264,128]{2,1,0:T(8,128)S(1)}, bf16[4,272,128]{2,1,0:T(8,128)(2,1)S(1)}, bf16[4,272,128]{2,1,0:T(8,128)(2,1)S(1)}, bf16[4,272,128]{2,1,0:T(8,128)(2,1)S(1)}) custom-call(s32[1]{0:T(128)} %bitcast.place_ref, s32[16,8]{1,0:T(8,128)S(1)} %copy.11.sel_ref, ...), custom_call_target="tpu_custom_call" | custom-call | flops 830472192 | bytes 4194304 | tf_op jit(solution)/shard_map/shared_head/pallas_call | solution.py:522
  107.1 1.4 collective-permute-start.37
  108.4 0.7 collective-permute-start.38
  109.1 7.7 %collective-permute-start.19 = (bf16[528,128]{1,0:T(8,128)(2,1)S(1)}, bf16[528,128]{1,0:T(8,128)(2,1)S(1)}, u32[]{:S(2)}, u32[]{:S(2)}) collective-permute-start(bf16[528,128]{1,0:T(8,128)(2,1)S(1)} %get-tuple-element.71), channel_id=1, source_target_pairs={{0,11},{1,10},{2,9},{3,8},{4,15},{5,14},{6,13},{7,12},{8,3},{9,2},... | collective-permute-start | bytes 405512 | tf_op jit(solution)/shard_map/ppermute | solution.py:503
  116.8 2.6 %collective-permute-start.20 = (bf16[528,128]{1,0:T(8,128)(2,1)S(1)}, bf16[528,128]{1,0:T(8,128)(2,1)S(1)}, u32[]{:S(2)}, u32[]{:S(2)}) collective-permute-start(bf16[528,128]{1,0:T(8,128)(2,1)S(1)} %get-tuple-element.72), channel_id=1, source_target_pairs={{0,10},{1,11},{2,8},{3,9},{4,14},{5,15},{6,12},{7,13},{8,2},{9,3},... | collective-permute-start | bytes 405512 | tf_op jit(solution)/shard_map/ppermute | solution.py:503
  119.4 7.7 %collective-permute-done.19.refs_4_ = bf16[528,128]{1,0:T(8,128)(2,1)S(1)} collective-permute-done((bf16[528,128]{1,0:T(8,128)(2,1)S(1)}, bf16[528,128]{1,0:T(8,128)(2,1)S(1)}, u32[]{:S(2)}, u32[]{:S(2)}) %collective-permute-start.19) | collective-permute-done | bytes 135200 | tf_op jit(solution)/shard_map/ppermute | solution.py:503
  127.2 2.9 %collective-permute-done.20.refs_5_ = bf16[528,128]{1,0:T(8,128)(2,1)S(1)} collective-permute-done((bf16[528,128]{1,0:T(8,128)(2,1)S(1)}, bf16[528,128]{1,0:T(8,128)(2,1)S(1)}, u32[]{:S(2)}, u32[]{:S(2)}) %collective-permute-start.20) | collective-permute-done | bytes 135200 | tf_op jit(solution)/shard_map/ppermute | solution.py:503
  130.3 7.1 %collective-permute-done.21.refs_6_ = bf16[528,128]{1,0:T(8,128)(2,1)S(1)} collective-permute-done((bf16[528,128]{1,0:T(8,128)(2,1)S(1)}, bf16[528,128]{1,0:T(8,128)(2,1)S(1)}, u32[]{:S(2)}, u32[]{:S(2)}) %collective-permute-start.21) | collective-permute-done | bytes 135200 | tf_op jit(solution)/shard_map/ppermute | solution.py:503
  137.5 3.3 %collective-permute-start.23 = (bf16[528,128]{1,0:T(8,128)(2,1)S(1)}, bf16[528,128]{1,0:T(8,128)(2,1)S(1)}, u32[]{:S(2)}, u32[]{:S(2)}) collective-permute-start(bf16[528,128]{1,0:T(8,128)(2,1)S(1)} %get-tuple-element.75), channel_id=1, source_target_pairs={{0,7},{1,6},{2,5},{3,4},{4,3},{5,2},{6,1},{7,0},{8,15},{9,14},{10,... | collective-permute-start | bytes 405512 | tf_op jit(solution)/shard_map/ppermute | solution.py:503
  140.7 1.2 collective-permute-done.22.refs_7_
  142.0 2.9 %collective-permute-start.25 = (bf16[528,128]{1,0:T(8,128)(2,1)S(1)}, bf16[528,128]{1,0:T(8,128)(2,1)S(1)}, u32[]{:S(2)}, u32[]{:S(2)}) collective-permute-start(bf16[528,128]{1,0:T(8,128)(2,1)S(1)} %get-tuple-element.77), channel_id=1, source_target_pairs={{0,5},{1,4},{2,7},{3,6},{4,1},{5,0},{6,3},{7,2},{8,13},{9,12},{10,... | collective-permute-start | bytes 405512 | tf_op jit(solution)/shard_map/ppermute | solution.py:503
  144.8 1.2 collective-permute-start.26
  146.9 0.8 collective-permute-done.24.refs_9_
  147.7 1.8 %collective-permute-start.29 = (bf16[528,128]{1,0:T(8,128)(2,1)S(1)}, bf16[528,128]{1,0:T(8,128)(2,1)S(1)}, u32[]{:S(2)}, u32[]{:S(2)}) collective-permute-start(bf16[528,128]{1,0:T(8,128)(2,1)S(1)} %get-tuple-element.81), channel_id=1, source_target_pairs={{0,1},{1,0},{2,3},{3,2},{4,5},{5,4},{6,7},{7,6},{8,9},{9,8},{10,11... | collective-permute-start | bytes 405512 | tf_op jit(solution)/shard_map/ppermute | solution.py:503
  149.6 2.3 %collective-permute-done.25.refs_10_ = bf16[528,128]{1,0:T(8,128)(2,1)S(1)} collective-permute-done((bf16[528,128]{1,0:T(8,128)(2,1)S(1)}, bf16[528,128]{1,0:T(8,128)(2,1)S(1)}, u32[]{:S(2)}, u32[]{:S(2)}) %collective-permute-start.25) | collective-permute-done | bytes 135200 | tf_op jit(solution)/shard_map/ppermute | solution.py:503
  151.9 2.4 %collective-permute-start.39 = (bf16[528,128]{1,0:T(8,128)(2,1)S(1)}, bf16[528,128]{1,0:T(8,128)(2,1)S(1)}, u32[]{:S(2)}, u32[]{:S(2)}) collective-permute-start(bf16[528,128]{1,0:T(8,128)(2,1)S(1)} %get-tuple-element.92), channel_id=1, source_target_pairs={{0,12},{1,13},{2,14},{3,15},{4,8},{5,9},{6,10},{7,11},{8,4},{9,5},... | collective-permute-start | bytes 405512 | tf_op jit(solution)/shard_map/ppermute | solution.py:503
  154.5 0.9 collective-permute-start.41
  155.4 3.7 %collective-permute-done.39.refs_16_ = bf16[528,128]{1,0:T(8,128)(2,1)S(1)} collective-permute-done((bf16[528,128]{1,0:T(8,128)(2,1)S(1)}, bf16[528,128]{1,0:T(8,128)(2,1)S(1)}, u32[]{:S(2)}, u32[]{:S(2)}) %collective-permute-start.39) | collective-permute-done | bytes 135200 | tf_op jit(solution)/shard_map/ppermute | solution.py:503
  159.1 6.8 %collective-permute-done.40.refs_17_ = bf16[528,128]{1,0:T(8,128)(2,1)S(1)} collective-permute-done((bf16[528,128]{1,0:T(8,128)(2,1)S(1)}, bf16[528,128]{1,0:T(8,128)(2,1)S(1)}, u32[]{:S(2)}, u32[]{:S(2)}) %collective-permute-start.40) | collective-permute-done | bytes 135200 | tf_op jit(solution)/shard_map/ppermute | solution.py:503
  166.0 2.0 %unpack.1 = (bf16[128,2560]{1,0:T(8,128)(2,1)}, bf16[128,2560]{1,0:T(8,128)(2,1)}, bf16[128,2560]{1,0:T(8,128)(2,1)}, bf16[128,2560]{1,0:T(8,128)(2,1)}, f32[2,2560]{1,0:T(2,128)}, /*index=5*/f32[2,2560]{1,0:T(2,128)}) custom-call(s32[1]{0:T(128)} %bitcast.place_ref, bf16[528,128]{1,0:T(8,128)(2,1)S(1)} %collective-permute-done.15.refs_0_, ...), custom_call_target="tpu_custom_call" | custom-call | tf_op jit(solution)/shard_map/unpack/pallas_call | solution.py:564
  (53 shorter events, 2.9 us)
Async XLA Ops:
  0.6 1.1 copy-start
  1.7 1.1 copy-start.1
  4.6 9.3 %copy-start.2 = (s32[16,8]{0,1:T(8,128)S(1)}, s32[16,8]{0,1:T(8,128)}, u32[]{:S(2)}) copy-start(s32[16,8]{0,1:T(8,128)} %param.9) | copy-start | bytes 1540
  4.6 9.4 %collective-permute-start = (bf16[512,128]{1,0:T(8,128)(2,1)S(1)}, bf16[512,128]{1,0:T(8,128)(2,1)S(1)}, u32[]{:S(2)}, u32[]{:S(2)}) collective-permute-start(bf16[512,128]{1,0:T(8,128)(2,1)S(1)} %get-tuple-element.51), channel_id=1, source_target_pairs={{0,15},{1,14},{2,13},{3,12},{4,11},{5,10},{6,9},{7,8},{8,7},{9,6},... | collective-permute-start | bytes 393224 | tf_op jit(solution)/shard_map/ppermute | solution.py:503
  10.3 16.9 %collective-permute-start.1 = (bf16[512,128]{1,0:T(8,128)(2,1)S(1)}, bf16[512,128]{1,0:T(8,128)(2,1)S(1)}, u32[]{:S(2)}, u32[]{:S(2)}) collective-permute-start(bf16[512,128]{1,0:T(8,128)(2,1)S(1)} %get-tuple-element.52), channel_id=1, source_target_pairs={{0,14},{1,15},{2,12},{3,13},{4,10},{5,11},{6,8},{7,9},{8,6},{9,7},... | collective-permute-start | bytes 393224 | tf_op jit(solution)/shard_map/ppermute | solution.py:503
  10.3 19.4 %collective-permute-start.2 = (bf16[512,128]{1,0:T(8,128)(2,1)S(1)}, bf16[512,128]{1,0:T(8,128)(2,1)S(1)}, u32[]{:S(2)}, u32[]{:S(2)}) collective-permute-start(bf16[512,128]{1,0:T(8,128)(2,1)S(1)} %get-tuple-element.53), channel_id=1, source_target_pairs={{0,13},{1,12},{2,15},{3,14},{4,9},{5,8},{6,11},{7,10},{8,5},{9,4},... | collective-permute-start | bytes 393224 | tf_op jit(solution)/shard_map/ppermute | solution.py:503
  13.5 26.8 %collective-permute-start.3 = (bf16[512,128]{1,0:T(8,128)(2,1)S(1)}, bf16[512,128]{1,0:T(8,128)(2,1)S(1)}, u32[]{:S(2)}, u32[]{:S(2)}) collective-permute-start(bf16[512,128]{1,0:T(8,128)(2,1)S(1)} %get-tuple-element.54), channel_id=1, source_target_pairs={{0,12},{1,13},{2,14},{3,15},{4,8},{5,9},{6,10},{7,11},{8,4},{9,5},... | collective-permute-start | bytes 393224 | tf_op jit(solution)/shard_map/ppermute | solution.py:503
  13.9 15.8 %collective-permute-start.30 = (bf16[512,128]{1,0:T(8,128)(2,1)S(1)}, bf16[512,128]{1,0:T(8,128)(2,1)S(1)}, u32[]{:S(2)}, u32[]{:S(2)}) collective-permute-start(bf16[512,128]{1,0:T(8,128)(2,1)S(1)} %get-tuple-element.84), channel_id=1, source_target_pairs={{0,4},{1,5},{2,6},{3,7},{4,0},{5,1},{6,2},{7,3},{8,12},{9,13},{10,... | collective-permute-start | bytes 393224 | tf_op jit(solution)/shard_map/ppermute | solution.py:503
  14.0 35.8 %collective-permute-start.4 = (bf16[512,128]{1,0:T(8,128)(2,1)S(1)}, bf16[512,128]{1,0:T(8,128)(2,1)S(1)}, u32[]{:S(2)}, u32[]{:S(2)}) collective-permute-start(bf16[512,128]{1,0:T(8,128)(2,1)S(1)} %get-tuple-element.55), channel_id=1, source_target_pairs={{0,11},{1,10},{2,9},{3,8},{4,15},{5,14},{6,13},{7,12},{8,3},{9,2},... | collective-permute-start | bytes 393224 | tf_op jit(solution)/shard_map/ppermute | solution.py:503
  27.2 25.4 %collective-permute-start.5 = (bf16[512,128]{1,0:T(8,128)(2,1)S(1)}, bf16[512,128]{1,0:T(8,128)(2,1)S(1)}, u32[]{:S(2)}, u32[]{:S(2)}) collective-permute-start(bf16[512,128]{1,0:T(8,128)(2,1)S(1)} %get-tuple-element.56), channel_id=1, source_target_pairs={{0,10},{1,11},{2,8},{3,9},{4,14},{5,15},{6,12},{7,13},{8,2},{9,3},... | collective-permute-start | bytes 393224 | tf_op jit(solution)/shard_map/ppermute | solution.py:503
  29.7 25.9 %collective-permute-start.31 = (bf16[512,128]{1,0:T(8,128)(2,1)S(1)}, bf16[512,128]{1,0:T(8,128)(2,1)S(1)}, u32[]{:S(2)}, u32[]{:S(2)}) collective-permute-start(bf16[512,128]{1,0:T(8,128)(2,1)S(1)} %get-tuple-element.85), channel_id=1, source_target_pairs={{0,8},{1,9},{2,10},{3,11},{4,12},{5,13},{6,14},{7,15},{8,0},{9,1},... | collective-permute-start | bytes 393224 | tf_op jit(solution)/shard_map/ppermute | solution.py:503
  29.7 28.7 %collective-permute-start.6 = (bf16[512,128]{1,0:T(8,128)(2,1)S(1)}, bf16[512,128]{1,0:T(8,128)(2,1)S(1)}, u32[]{:S(2)}, u32[]{:S(2)}) collective-permute-start(bf16[512,128]{1,0:T(8,128)(2,1)S(1)} %get-tuple-element.57), channel_id=1, source_target_pairs={{0,9},{1,8},{2,11},{3,10},{4,13},{5,12},{6,15},{7,14},{8,1},{9,0},... | collective-permute-start | bytes 393224 | tf_op jit(solution)/shard_map/ppermute | solution.py:503
  40.3 23.7 %collective-permute-start.7 = (bf16[512,128]{1,0:T(8,128)(2,1)S(1)}, bf16[512,128]{1,0:T(8,128)(2,1)S(1)}, u32[]{:S(2)}, u32[]{:S(2)}) collective-permute-start(bf16[512,128]{1,0:T(8,128)(2,1)S(1)} %get-tuple-element.58), channel_id=1, source_target_pairs={{0,8},{1,9},{2,10},{3,11},{4,12},{5,13},{6,14},{7,15},{8,0},{9,1},... | collective-permute-start | bytes 393224 | tf_op jit(solution)/shard_map/ppermute | solution.py:503
  49.8 17.0 %collective-permute-start.8 = (bf16[512,128]{1,0:T(8,128)(2,1)S(1)}, bf16[512,128]{1,0:T(8,128)(2,1)S(1)}, u32[]{:S(2)}, u32[]{:S(2)}) collective-permute-start(bf16[512,128]{1,0:T(8,128)(2,1)S(1)} %get-tuple-element.59), channel_id=1, source_target_pairs={{0,7},{1,6},{2,5},{3,4},{4,3},{5,2},{6,1},{7,0},{8,15},{9,14},{10,... | collective-permute-start | bytes 393224 | tf_op jit(solution)/shard_map/ppermute | solution.py:503
  52.6 17.0 %collective-permute-start.9 = (bf16[512,128]{1,0:T(8,128)(2,1)S(1)}, bf16[512,128]{1,0:T(8,128)(2,1)S(1)}, u32[]{:S(2)}, u32[]{:S(2)}) collective-permute-start(bf16[512,128]{1,0:T(8,128)(2,1)S(1)} %get-tuple-element.60), channel_id=1, source_target_pairs={{0,6},{1,7},{2,4},{3,5},{4,2},{5,3},{6,0},{7,1},{8,14},{9,15},{10,... | collective-permute-start | bytes 393224 | tf_op jit(solution)/shard_map/ppermute | solution.py:503
  55.6 15.2 %collective-permute-start.32 = (bf16[512,128]{1,0:T(8,128)(2,1)S(1)}, bf16[512,128]{1,0:T(8,128)(2,1)S(1)}, u32[]{:S(2)}, u32[]{:S(2)}) collective-permute-start(bf16[512,128]{1,0:T(8,128)(2,1)S(1)} %get-tuple-element.86), channel_id=1, source_target_pairs={{0,12},{1,13},{2,14},{3,15},{4,8},{5,9},{6,10},{7,11},{8,4},{9,5},... | collective-permute-start | bytes 393224 | tf_op jit(solution)/shard_map/ppermute | solution.py:503
  58.5 14.0 %collective-permute-start.10 = (bf16[512,128]{1,0:T(8,128)(2,1)S(1)}, bf16[512,128]{1,0:T(8,128)(2,1)S(1)}, u32[]{:S(2)}, u32[]{:S(2)}) collective-permute-start(bf16[512,128]{1,0:T(8,128)(2,1)S(1)} %get-tuple-element.61), channel_id=1, source_target_pairs={{0,5},{1,4},{2,7},{3,6},{4,1},{5,0},{6,3},{7,2},{8,13},{9,12},{10,... | collective-permute-start | bytes 393224 | tf_op jit(solution)/shard_map/ppermute | solution.py:503
  64.1 11.2 %collective-permute-start.11 = (bf16[512,128]{1,0:T(8,128)(2,1)S(1)}, bf16[512,128]{1,0:T(8,128)(2,1)S(1)}, u32[]{:S(2)}, u32[]{:S(2)}) collective-permute-start(bf16[512,128]{1,0:T(8,128)(2,1)S(1)} %get-tuple-element.62), channel_id=1, source_target_pairs={{0,4},{1,5},{2,6},{3,7},{4,0},{5,1},{6,2},{7,3},{8,12},{9,13},{10,... | collective-permute-start | bytes 393224 | tf_op jit(solution)/shard_map/ppermute | solution.py:503
  66.8 8.7 %collective-permute-start.12 = (bf16[512,128]{1,0:T(8,128)(2,1)S(1)}, bf16[512,128]{1,0:T(8,128)(2,1)S(1)}, u32[]{:S(2)}, u32[]{:S(2)}) collective-permute-start(bf16[512,128]{1,0:T(8,128)(2,1)S(1)} %get-tuple-element.63), channel_id=1, source_target_pairs={{0,3},{1,2},{2,1},{3,0},{4,7},{5,6},{6,5},{7,4},{8,11},{9,10},{10,... | collective-permute-start | bytes 393224 | tf_op jit(solution)/shard_map/ppermute | solution.py:503
  69.6 6.6 %collective-permute-start.13 = (bf16[512,128]{1,0:T(8,128)(2,1)S(1)}, bf16[512,128]{1,0:T(8,128)(2,1)S(1)}, u32[]{:S(2)}, u32[]{:S(2)}) collective-permute-start(bf16[512,128]{1,0:T(8,128)(2,1)S(1)} %get-tuple-element.64), channel_id=1, source_target_pairs={{0,2},{1,3},{2,0},{3,1},{4,6},{5,7},{6,4},{7,5},{8,10},{9,11},{10,... | collective-permute-start | bytes 393224 | tf_op jit(solution)/shard_map/ppermute | solution.py:503
  70.8 5.4 %collective-permute-start.14 = (bf16[512,128]{1,0:T(8,128)(2,1)S(1)}, bf16[512,128]{1,0:T(8,128)(2,1)S(1)}, u32[]{:S(2)}, u32[]{:S(2)}) collective-permute-start(bf16[512,128]{1,0:T(8,128)(2,1)S(1)} %get-tuple-element.65), channel_id=1, source_target_pairs={{0,1},{1,0},{2,3},{3,2},{4,5},{5,4},{6,7},{7,6},{8,9},{9,8},{10,11... | collective-permute-start | bytes 393224 | tf_op jit(solution)/shard_map/ppermute | solution.py:503
  72.4 24.5 %collective-permute-start.35 = (bf16[4,256,128]{2,1,0:T(8,128)(2,1)S(1)}, bf16[4,256,128]{2,1,0:T(8,128)(2,1)S(1)}, u32[]{:S(2)}, u32[]{:S(2)}) collective-permute-start(bf16[4,256,128]{2,1,0:T(8,128)(2,1)S(1)} %pad_maximum_fusion), channel_id=1, source_target_pairs={{0,3},{1,2},{2,1},{3,0},{4,7},{5,6},{6,5},{7,4},{8,11},{9,10},{10,... | collective-permute-start | bytes 786440 | tf_op jit(solution)/shard_map/ppermute | solution.py:503
  75.3 24.5 %collective-permute-start.34 = (bf16[4,256,128]{2,1,0:T(8,128)(2,1)S(1)}, bf16[4,256,128]{2,1,0:T(8,128)(2,1)S(1)}, u32[]{:S(2)}, u32[]{:S(2)}) collective-permute-start(bf16[4,256,128]{2,1,0:T(8,128)(2,1)S(1)} %pad_maximum_fusion), channel_id=1, source_target_pairs={{0,2},{1,3},{2,0},{3,1},{4,6},{5,7},{6,4},{7,5},{8,10},{9,11},{10,... | collective-permute-start | bytes 786440 | tf_op jit(solution)/shard_map/ppermute | solution.py:503
  75.5 25.3 %collective-permute-start.33 = (bf16[4,256,128]{2,1,0:T(8,128)(2,1)S(1)}, bf16[4,256,128]{2,1,0:T(8,128)(2,1)S(1)}, u32[]{:S(2)}, u32[]{:S(2)}) collective-permute-start(bf16[4,256,128]{2,1,0:T(8,128)(2,1)S(1)} %pad_maximum_fusion), channel_id=1, source_target_pairs={{0,1},{1,0},{2,3},{3,2},{4,5},{5,4},{6,7},{7,6},{8,9},{9,8},{10,11... | collective-permute-start | bytes 786440 | tf_op jit(solution)/shard_map/ppermute | solution.py:503
  92.8 14.3 %collective-permute-start.15 = (bf16[528,128]{1,0:T(8,128)(2,1)}, bf16[528,128]{1,0:T(8,128)(2,1)S(1)}, u32[]{:S(2)}, u32[]{:S(2)}) collective-permute-start(bf16[528,128]{1,0:T(8,128)(2,1)} %get-tuple-element.67), channel_id=1, source_target_pairs={{0,15},{1,14},{2,13},{3,12},{4,11},{5,10},{6,9},{7,8},{8,7},{9,6},... | collective-permute-start | bytes 405512 | tf_op jit(solution)/shard_map/ppermute | solution.py:503
  96.0 12.4 %collective-permute-start.16 = (bf16[528,128]{1,0:T(8,128)(2,1)}, bf16[528,128]{1,0:T(8,128)(2,1)S(1)}, u32[]{:S(2)}, u32[]{:S(2)}) collective-permute-start(bf16[528,128]{1,0:T(8,128)(2,1)} %get-tuple-element.68), channel_id=1, source_target_pairs={{0,14},{1,15},{2,12},{3,13},{4,10},{5,11},{6,8},{7,9},{8,6},{9,7},... | collective-permute-start | bytes 405512 | tf_op jit(solution)/shard_map/ppermute | solution.py:503
  96.9 12.2 %collective-permute-start.17 = (bf16[528,128]{1,0:T(8,128)(2,1)S(1)}, bf16[528,128]{1,0:T(8,128)(2,1)S(1)}, u32[]{:S(2)}, u32[]{:S(2)}) collective-permute-start(bf16[528,128]{1,0:T(8,128)(2,1)S(1)} %get-tuple-element.69), channel_id=1, source_target_pairs={{0,13},{1,12},{2,15},{3,14},{4,9},{5,8},{6,11},{7,10},{8,5},{9,4},... | collective-permute-start | bytes 405512 | tf_op jit(solution)/shard_map/ppermute | solution.py:503
  99.7 17.1 %collective-permute-start.18 = (bf16[528,128]{1,0:T(8,128)(2,1)S(1)}, bf16[528,128]{1,0:T(8,128)(2,1)S(1)}, u32[]{:S(2)}, u32[]{:S(2)}) collective-permute-start(bf16[528,128]{1,0:T(8,128)(2,1)S(1)} %get-tuple-element.70), channel_id=1, source_target_pairs={{0,12},{1,13},{2,14},{3,15},{4,8},{5,9},{6,10},{7,11},{8,4},{9,5},... | collective-permute-start | bytes 405512 | tf_op jit(solution)/shard_map/ppermute | solution.py:503
  106.9 35.0 %collective-permute-start.36 = (bf16[4,272,128]{2,1,0:T(8,128)(2,1)S(1)}, bf16[4,272,128]{2,1,0:T(8,128)(2,1)S(1)}, u32[]{:S(2)}, u32[]{:S(2)}) collective-permute-start(bf16[4,272,128]{2,1,0:T(8,128)(2,1)S(1)} %get-tuple-element.89), channel_id=1, source_target_pairs={{0,1},{1,0},{2,3},{3,2},{4,5},{5,4},{6,7},{7,6},{8,9},{9,8},{10,11... | collective-permute-start | bytes 835592 | tf_op jit(solution)/shard_map/ppermute | solution.py:503
  107.1 37.8 %collective-permute-start.37 = (bf16[4,272,128]{2,1,0:T(8,128)(2,1)S(1)}, bf16[4,272,128]{2,1,0:T(8,128)(2,1)S(1)}, u32[]{:S(2)}, u32[]{:S(2)}) collective-permute-start(bf16[4,272,128]{2,1,0:T(8,128)(2,1)S(1)} %get-tuple-element.90), channel_id=1, source_target_pairs={{0,2},{1,3},{2,0},{3,1},{4,6},{5,7},{6,4},{7,5},{8,10},{9,11},{10,... | collective-permute-start | bytes 835592 | tf_op jit(solution)/shard_map/ppermute | solution.py:503
  108.4 37.7 %collective-permute-start.38 = (bf16[4,272,128]{2,1,0:T(8,128)(2,1)S(1)}, bf16[4,272,128]{2,1,0:T(8,128)(2,1)S(1)}, u32[]{:S(2)}, u32[]{:S(2)}) collective-permute-start(bf16[4,272,128]{2,1,0:T(8,128)(2,1)S(1)} %get-tuple-element.91), channel_id=1, source_target_pairs={{0,3},{1,2},{2,1},{3,0},{4,7},{5,6},{6,5},{7,4},{8,11},{9,10},{10,... | collective-permute-start | bytes 835592 | tf_op jit(solution)/shard_map/ppermute | solution.py:503
  109.1 18.0 %collective-permute-start.19 = (bf16[528,128]{1,0:T(8,128)(2,1)S(1)}, bf16[528,128]{1,0:T(8,128)(2,1)S(1)}, u32[]{:S(2)}, u32[]{:S(2)}) collective-permute-start(bf16[528,128]{1,0:T(8,128)(2,1)S(1)} %get-tuple-element.71), channel_id=1, source_target_pairs={{0,11},{1,10},{2,9},{3,8},{4,15},{5,14},{6,13},{7,12},{8,3},{9,2},... | collective-permute-start | bytes 405512 | tf_op jit(solution)/shard_map/ppermute | solution.py:503
  116.8 13.3 %collective-permute-start.20 = (bf16[528,128]{1,0:T(8,128)(2,1)S(1)}, bf16[528,128]{1,0:T(8,128)(2,1)S(1)}, u32[]{:S(2)}, u32[]{:S(2)}) collective-permute-start(bf16[528,128]{1,0:T(8,128)(2,1)S(1)} %get-tuple-element.72), channel_id=1, source_target_pairs={{0,10},{1,11},{2,8},{3,9},{4,14},{5,15},{6,12},{7,13},{8,2},{9,3},... | collective-permute-start | bytes 405512 | tf_op jit(solution)/shard_map/ppermute | solution.py:503
  127.2 10.3 %collective-permute-start.21 = (bf16[528,128]{1,0:T(8,128)(2,1)S(1)}, bf16[528,128]{1,0:T(8,128)(2,1)S(1)}, u32[]{:S(2)}, u32[]{:S(2)}) collective-permute-start(bf16[528,128]{1,0:T(8,128)(2,1)S(1)} %get-tuple-element.73), channel_id=1, source_target_pairs={{0,9},{1,8},{2,11},{3,10},{4,13},{5,12},{6,15},{7,14},{8,1},{9,0},... | collective-permute-start | bytes 405512 | tf_op jit(solution)/shard_map/ppermute | solution.py:503
  130.1 11.9 %collective-permute-start.22 = (bf16[528,128]{1,0:T(8,128)(2,1)S(1)}, bf16[528,128]{1,0:T(8,128)(2,1)S(1)}, u32[]{:S(2)}, u32[]{:S(2)}) collective-permute-start(bf16[528,128]{1,0:T(8,128)(2,1)S(1)} %get-tuple-element.74), channel_id=1, source_target_pairs={{0,8},{1,9},{2,10},{3,11},{4,12},{5,13},{6,14},{7,15},{8,0},{9,1},... | collective-permute-start | bytes 405512 | tf_op jit(solution)/shard_map/ppermute | solution.py:503
  137.5 8.8 %collective-permute-start.23 = (bf16[528,128]{1,0:T(8,128)(2,1)S(1)}, bf16[528,128]{1,0:T(8,128)(2,1)S(1)}, u32[]{:S(2)}, u32[]{:S(2)}) collective-permute-start(bf16[528,128]{1,0:T(8,128)(2,1)S(1)} %get-tuple-element.75), channel_id=1, source_target_pairs={{0,7},{1,6},{2,5},{3,4},{4,3},{5,2},{6,1},{7,0},{8,15},{9,14},{10,... | collective-permute-start | bytes 405512 | tf_op jit(solution)/shard_map/ppermute | solution.py:503
  141.9 5.8 %collective-permute-start.24 = (bf16[528,128]{1,0:T(8,128)(2,1)S(1)}, bf16[528,128]{1,0:T(8,128)(2,1)S(1)}, u32[]{:S(2)}, u32[]{:S(2)}) collective-permute-start(bf16[528,128]{1,0:T(8,128)(2,1)S(1)} %get-tuple-element.76), channel_id=1, source_target_pairs={{0,6},{1,7},{2,4},{3,5},{4,2},{5,3},{6,0},{7,1},{8,14},{9,15},{10,... | collective-permute-start | bytes 405512 | tf_op jit(solution)/shard_map/ppermute | solution.py:503
  142.0 9.9 %collective-permute-start.25 = (bf16[528,128]{1,0:T(8,128)(2,1)S(1)}, bf16[528,128]{1,0:T(8,128)(2,1)S(1)}, u32[]{:S(2)}, u32[]{:S(2)}) collective-permute-start(bf16[528,128]{1,0:T(8,128)(2,1)S(1)} %get-tuple-element.77), channel_id=1, source_target_pairs={{0,5},{1,4},{2,7},{3,6},{4,1},{5,0},{6,3},{7,2},{8,13},{9,12},{10,... | collective-permute-start | bytes 405512 | tf_op jit(solution)/shard_map/ppermute | solution.py:503
  144.8 9.4 %collective-permute-start.26 = (bf16[528,128]{1,0:T(8,128)(2,1)S(1)}, bf16[528,128]{1,0:T(8,128)(2,1)S(1)}, u32[]{:S(2)}, u32[]{:S(2)}) collective-permute-start(bf16[528,128]{1,0:T(8,128)(2,1)S(1)} %get-tuple-element.78), channel_id=1, source_target_pairs={{0,4},{1,5},{2,6},{3,7},{4,0},{5,1},{6,2},{7,3},{8,12},{9,13},{10,... | collective-permute-start | bytes 405512 | tf_op jit(solution)/shard_map/ppermute | solution.py:503
  146.1 8.5 %collective-permute-start.27 = (bf16[528,128]{1,0:T(8,128)(2,1)S(1)}, bf16[528,128]{1,0:T(8,128)(2,1)S(1)}, u32[]{:S(2)}, u32[]{:S(2)}) collective-permute-start(bf16[528,128]{1,0:T(8,128)(2,1)S(1)} %get-tuple-element.79), channel_id=1, source_target_pairs={{0,3},{1,2},{2,1},{3,0},{4,7},{5,6},{6,5},{7,4},{8,11},{9,10},{10,... | collective-permute-start | bytes 405512 | tf_op jit(solution)/shard_map/ppermute | solution.py:503
  146.2 9.2 %collective-permute-start.28 = (bf16[528,128]{1,0:T(8,128)(2,1)S(1)}, bf16[528,128]{1,0:T(8,128)(2,1)S(1)}, u32[]{:S(2)}, u32[]{:S(2)}) collective-permute-start(bf16[528,128]{1,0:T(8,128)(2,1)S(1)} %get-tuple-element.80), channel_id=1, source_target_pairs={{0,2},{1,3},{2,0},{3,1},{4,6},{5,7},{6,4},{7,5},{8,10},{9,11},{10,... | collective-permute-start | bytes 405512 | tf_op jit(solution)/shard_map/ppermute | solution.py:503
  147.7 7.7 %collective-permute-start.29 = (bf16[528,128]{1,0:T(8,128)(2,1)S(1)}, bf16[528,128]{1,0:T(8,128)(2,1)S(1)}, u32[]{:S(2)}, u32[]{:S(2)}) collective-permute-start(bf16[528,128]{1,0:T(8,128)(2,1)S(1)} %get-tuple-element.81), channel_id=1, source_target_pairs={{0,1},{1,0},{2,3},{3,2},{4,5},{5,4},{6,7},{7,6},{8,9},{9,8},{10,11... | collective-permute-start | bytes 405512 | tf_op jit(solution)/shard_map/ppermute | solution.py:503
  151.9 7.3 %collective-permute-start.39 = (bf16[528,128]{1,0:T(8,128)(2,1)S(1)}, bf16[528,128]{1,0:T(8,128)(2,1)S(1)}, u32[]{:S(2)}, u32[]{:S(2)}) collective-permute-start(bf16[528,128]{1,0:T(8,128)(2,1)S(1)} %get-tuple-element.92), channel_id=1, source_target_pairs={{0,12},{1,13},{2,14},{3,15},{4,8},{5,9},{6,10},{7,11},{8,4},{9,5},... | collective-permute-start | bytes 405512 | tf_op jit(solution)/shard_map/ppermute | solution.py:503
  154.3 11.7 %collective-permute-start.40 = (bf16[528,128]{1,0:T(8,128)(2,1)S(1)}, bf16[528,128]{1,0:T(8,128)(2,1)S(1)}, u32[]{:S(2)}, u32[]{:S(2)}) collective-permute-start(bf16[528,128]{1,0:T(8,128)(2,1)S(1)} %get-tuple-element.93), channel_id=1, source_target_pairs={{0,8},{1,9},{2,10},{3,11},{4,12},{5,13},{6,14},{7,15},{8,0},{9,1},... | collective-permute-start | bytes 405512 | tf_op jit(solution)/shard_map/ppermute | solution.py:503
  154.5 11.5 %collective-permute-start.41 = (bf16[528,128]{1,0:T(8,128)(2,1)S(1)}, bf16[528,128]{1,0:T(8,128)(2,1)S(1)}, u32[]{:S(2)}, u32[]{:S(2)}) collective-permute-start(bf16[528,128]{1,0:T(8,128)(2,1)S(1)} %get-tuple-element.94), channel_id=1, source_target_pairs={{0,4},{1,5},{2,6},{3,7},{4,0},{5,1},{6,2},{7,3},{8,12},{9,13},{10,... | collective-permute-start | bytes 405512 | tf_op jit(solution)/shard_map/ppermute | solution.py:503

commit v3 on v2

--- a/solution.py
+++ b/solution.py
@@ -215,26 +215,30 @@
     return pl.ds(pl.multiple_of(index * LANES, LANES), LANES)
 
 
-def pack_body(heads, span, place_ref, q_ref, k_ref, v_ref, g_ref, *out_refs):
-    place = place_ref[0]
+def pack_body(first, place_ref, q_ref, k_ref, v_ref, g_ref, *out_refs):
     for step, out_ref in enumerate(out_refs):
-        if step < heads:
-            head = lax.bitwise_xor(place, step)
-        else:
-            head = heads + lax.bitwise_xor(place // span, step - heads)
+        columns = lane_block(first + lax.bitwise_xor(place_ref[0], step))
         for index, ref in enumerate((q_ref, k_ref, v_ref, g_ref)):
-            out_ref[index * TILE : (index + 1) * TILE, :] = ref[:, lane_block(head)]
-
-
-def pack(arrays, place, devices, span):
+            out_ref[index * TILE : (index + 1) * TILE, :] = ref[:, columns]
+
+
+def pack(arrays, place, first, count):
+    width = arrays[0].shape[1]
+    if first % count == 0:
+        spec = pl.BlockSpec((TILE, count * LANES), lambda i, _: (0, first // count))
+        start = 0
+    else:
+        spec = pl.BlockSpec((TILE, width), lambda i, _: (0, 0))
+        start = first
+    out = pl.BlockSpec((4 * TILE, LANES), lambda i, _: (0, 0))
     return pl.pallas_call(
-        functools.partial(pack_body, devices, span),
-        in_specs=[SMEM] + [VMEM] * 4,
-        out_specs=[VMEM] * HEADS,
-        out_shape=[jax.ShapeDtypeStruct((4 * TILE, LANES), jnp.bfloat16)] * HEADS,
-        compiler_params=BIG,
+        functools.partial(pack_body, start),
+        grid_spec=pltpu.PrefetchScalarGridSpec(
+            num_scalar_prefetch=1, grid=(1,), in_specs=[spec] * 4, out_specs=[out] * count
+        ),
+        out_shape=[jax.ShapeDtypeStruct((4 * TILE, LANES), jnp.bfloat16)] * count,
         cost_estimate=pl.CostEstimate(
-            flops=0, transcendentals=0, bytes_accessed=16 * HEADS * TILE * LANES
+            flops=0, transcendentals=0, bytes_accessed=16 * count * TILE * LANES
         ),
         name="pack",
     )(place, *arrays)
@@ -514,9 +518,8 @@
     block = 4 * TILE + tail_height()
     part = 2 * TILE + tail_height()
     keys = SEL * TILE + devices * (TILE // POOL)
-    packed = pack(arrays, place, devices, span)
-    owns = spread(packed[devices:], span)
-    mains = spread(packed[:devices], 1)
+    owns = spread(pack(arrays, place // span, devices, planes), span)
+    mains = spread(pack(arrays, place, 0, devices), 1)
     own_kv = jnp.stack([own[TILE : 3 * TILE] for own in owns])
     pieces = [shift(own_kv, step) for step in range(1, span)]
     outs = pl.pallas_call(

time: 168 us -> 168 us (level)
  waiting for transfers between devices: 58.9 us -> 45 us
  starting transfers between devices: 79.4 us -> 91.1 us
  Pallas kernels: 26.6 us -> 30.3 us
  local copies, waits for them, and re-layouts: 2.27 us -> 0.11 us
    ppermute x42, waiting for transfers between devices: 58.9 us -> 45 us  [shift(): return lax.ppermute(block, 'ctx', [(i, i ^ step) for i in range(devices)])]
    ppermute x42, starting transfers between devices: 79.4 us -> 91.1 us  [shift(): return lax.ppermute(block, 'ctx', [(i, i ^ step) for i in range(devices)])]
    pallas_call x1 -> x2, Pallas kernels: 1.76 us -> 5.41 us  [pack(): pl.pallas_call(functools.partial(pack_body, start), grid_spec=pltpu.Prefe...]
    unnamed x7 -> x13, local copies, waits for them, and re-layouts: 2.24 us -> 0.09 us
  transfers between devices with their start and end apart: 42 -> 42, of which waited for: 17 -> 16; matrix products, arithmetic and copies ran while one was open for 0% -> 0% of each run, Pallas kernels for 14% -> 16%
where the time goes in v3:
time: 168 us; the launch traced here: 167 us
  starting transfers between devices  91.1 us (54%)
  waiting for transfers between devices  45 us (27%)
  Pallas kernels  30.3 us (18%)
    ppermute x42, starting transfers between devices, shift(): return lax.ppermute(block, 'ctx', [(i, i ^ step) for i in range(devices)])  91.1 us
    ppermute x42, waiting for transfers between devices, shift(): return lax.ppermute(block, 'ctx', [(i, i ^ step) for i in range(devices)])  45 us
    pallas_call x1, Pallas kernels, head_shards(): pl.pallas_call(functools.partial(whole_head, devices), in_specs=[SMEM, SM...  16.6 us
    pallas_call x1, Pallas kernels, head_shards(): pl.pallas_call(functools.partial(shared_head, span, planes), in_specs=[SM...  6.12 us
    pallas_call x2, Pallas kernels, pack(): pl.pallas_call(functools.partial(pack_body, start), grid_spec=pltpu.Prefe...  5.41 us
  transfers between devices with their start and end apart: 42, of which 16 were waited for; matrix products, arithmetic and copies ran while one was open for 0% of the time, Pallas kernels for 16%

profile of v3, /device:TPU:1, one launch (start us, length us, event | category | flops | bytes accessed | tf_op | source)
XLA Modules:
  0.0 167.2 jit_solution(1161834835604214930)
XLA Ops:
  0.6 2.0 %pack.3 = (bf16[512,128]{1,0:T(8,128)(2,1)}, bf16[512,128]{1,0:T(8,128)(2,1)}, bf16[512,128]{1,0:T(8,128)(2,1)}, bf16[512,128]{1,0:T(8,128)(2,1)}) custom-call(s32[1]{0:T(128)S(6)} %select_n.5.place_ref, bf16[128,2560]{1,0:T(8,128)(2,1)} %q_ref.3, bf16[128,2560]{1,0:T(8,128)(2,1)} %k_ref.3, bf16[128,2560]{1,0:T(8,128)(2,1)} %v_ref.3, bf16[128,2560]{1,0:T(8,128)(2,1)} %g_ref.3), custom_call_target="tpu_custom_call" | custom-call | bytes 1048576 | tf_op jit(solution)/shard_map/pack/pallas_call | solution.py:234
  2.6 2.1 %collective-permute-start.30 = (bf16[512,128]{1,0:T(8,128)(2,1)}, bf16[512,128]{1,0:T(8,128)(2,1)S(1)}, u32[]{:S(2)}, u32[]{:S(2)}) collective-permute-start(bf16[512,128]{1,0:T(8,128)(2,1)} %get-tuple-element.84), channel_id=1, source_target_pairs={{0,4},{1,5},{2,6},{3,7},{4,0},{5,1},{6,2},{7,3},{8,12},{9,13},{10,... | collective-permute-start | bytes 393224 | tf_op jit(solution)/shard_map/ppermute | solution.py:507
  4.8 2.3 %collective-permute-start.31 = (bf16[512,128]{1,0:T(8,128)(2,1)}, bf16[512,128]{1,0:T(8,128)(2,1)S(1)}, u32[]{:S(2)}, u32[]{:S(2)}) collective-permute-start(bf16[512,128]{1,0:T(8,128)(2,1)} %get-tuple-element.85), channel_id=1, source_target_pairs={{0,8},{1,9},{2,10},{3,11},{4,12},{5,13},{6,14},{7,15},{8,0},{9,1},... | collective-permute-start | bytes 393224 | tf_op jit(solution)/shard_map/ppermute | solution.py:507
  7.1 3.4 %pack.2 = (bf16[512,128]{1,0:T(8,128)(2,1)}, bf16[512,128]{1,0:T(8,128)(2,1)}, bf16[512,128]{1,0:T(8,128)(2,1)}, bf16[512,128]{1,0:T(8,128)(2,1)}, bf16[512,128]...) custom-call(s32[1]{0:T(128)} %bitcast.place_ref, ...), custom_call_target="tpu_custom_call" | custom-call | bytes 4194304 | tf_op jit(solution)/shard_map/pack/pallas_call | solution.py:234
  10.5 5.6 %collective-permute-start = (bf16[512,128]{1,0:T(8,128)(2,1)}, bf16[512,128]{1,0:T(8,128)(2,1)S(1)}, u32[]{:S(2)}, u32[]{:S(2)}) collective-permute-start(bf16[512,128]{1,0:T(8,128)(2,1)} %get-tuple-element.51), channel_id=1, source_target_pairs={{0,15},{1,14},{2,13},{3,12},{4,11},{5,10},{6,9},{7,8},{8,7},{9,6},... | collective-permute-start | bytes 393224 | tf_op jit(solution)/shard_map/ppermute | solution.py:507
  16.2 2.5 %collective-permute-start.2 = (bf16[512,128]{1,0:T(8,128)(2,1)}, bf16[512,128]{1,0:T(8,128)(2,1)S(1)}, u32[]{:S(2)}, u32[]{:S(2)}) collective-permute-start(bf16[512,128]{1,0:T(8,128)(2,1)} %get-tuple-element.53), channel_id=1, source_target_pairs={{0,13},{1,12},{2,15},{3,14},{4,9},{5,8},{6,11},{7,10},{8,5},{9,4},... | collective-permute-start | bytes 393224 | tf_op jit(solution)/shard_map/ppermute | solution.py:507
  18.6 1.2 collective-permute-start.3
  19.9 13.5 %collective-permute-start.4 = (bf16[512,128]{1,0:T(8,128)(2,1)}, bf16[512,128]{1,0:T(8,128)(2,1)S(1)}, u32[]{:S(2)}, u32[]{:S(2)}) collective-permute-start(bf16[512,128]{1,0:T(8,128)(2,1)} %get-tuple-element.55), channel_id=1, source_target_pairs={{0,11},{1,10},{2,9},{3,8},{4,15},{5,14},{6,13},{7,12},{8,3},{9,2},... | collective-permute-start | bytes 393224 | tf_op jit(solution)/shard_map/ppermute | solution.py:507
  33.4 2.2 %collective-permute-start.5 = (bf16[512,128]{1,0:T(8,128)(2,1)}, bf16[512,128]{1,0:T(8,128)(2,1)S(1)}, u32[]{:S(2)}, u32[]{:S(2)}) collective-permute-start(bf16[512,128]{1,0:T(8,128)(2,1)} %get-tuple-element.56), channel_id=1, source_target_pairs={{0,10},{1,11},{2,8},{3,9},{4,14},{5,15},{6,12},{7,13},{8,2},{9,3},... | collective-permute-start | bytes 393224 | tf_op jit(solution)/shard_map/ppermute | solution.py:507
  35.6 10.4 %collective-permute-start.6 = (bf16[512,128]{1,0:T(8,128)(2,1)}, bf16[512,128]{1,0:T(8,128)(2,1)S(1)}, u32[]{:S(2)}, u32[]{:S(2)}) collective-permute-start(bf16[512,128]{1,0:T(8,128)(2,1)} %get-tuple-element.57), channel_id=1, source_target_pairs={{0,9},{1,8},{2,11},{3,10},{4,13},{5,12},{6,15},{7,14},{8,1},{9,0},... | collective-permute-start | bytes 393224 | tf_op jit(solution)/shard_map/ppermute | solution.py:507
  46.0 1.3 collective-permute-start.7
  47.3 8.2 %collective-permute-start.8 = (bf16[512,128]{1,0:T(8,128)(2,1)}, bf16[512,128]{1,0:T(8,128)(2,1)S(1)}, u32[]{:S(2)}, u32[]{:S(2)}) collective-permute-start(bf16[512,128]{1,0:T(8,128)(2,1)} %get-tuple-element.59), channel_id=1, source_target_pairs={{0,7},{1,6},{2,5},{3,4},{4,3},{5,2},{6,1},{7,0},{8,15},{9,14},{10,... | collective-permute-start | bytes 393224 | tf_op jit(solution)/shard_map/ppermute | solution.py:507
  55.5 3.0 %collective-permute-done.4.refs_4_ = bf16[512,128]{1,0:T(8,128)(2,1)S(1)} collective-permute-done((bf16[512,128]{1,0:T(8,128)(2,1)}, bf16[512,128]{1,0:T(8,128)(2,1)S(1)}, u32[]{:S(2)}, u32[]{:S(2)}) %collective-permute-start.4) | collective-permute-done | bytes 131104 | tf_op jit(solution)/shard_map/ppermute | solution.py:507
  58.5 0.3 collective-permute-done.5.refs_5_
  58.7 1.4 collective-permute-start.10
  60.2 3.0 %collective-permute-done.6.refs_6_ = bf16[512,128]{1,0:T(8,128)(2,1)S(1)} collective-permute-done((bf16[512,128]{1,0:T(8,128)(2,1)}, bf16[512,128]{1,0:T(8,128)(2,1)S(1)}, u32[]{:S(2)}, u32[]{:S(2)}) %collective-permute-start.6) | collective-permute-done | bytes 131104 | tf_op jit(solution)/shard_map/ppermute | solution.py:507
  63.5 2.9 %collective-permute-start.12 = (bf16[512,128]{1,0:T(8,128)(2,1)S(1)}, bf16[512,128]{1,0:T(8,128)(2,1)S(1)}, u32[]{:S(2)}, u32[]{:S(2)}) collective-permute-start(bf16[512,128]{1,0:T(8,128)(2,1)S(1)} %copy-done.5), channel_id=1, source_target_pairs={{0,3},{1,2},{2,1},{3,0},{4,7},{5,6},{6,5},{7,4},{8,11},{9,10},{10,... | collective-permute-start | bytes 393224 | tf_op jit(solution)/shard_map/ppermute | solution.py:507
  66.4 1.8 %collective-permute-done.8.refs_8_ = bf16[512,128]{1,0:T(8,128)(2,1)S(1)} collective-permute-done((bf16[512,128]{1,0:T(8,128)(2,1)}, bf16[512,128]{1,0:T(8,128)(2,1)S(1)}, u32[]{:S(2)}, u32[]{:S(2)}) %collective-permute-start.8) | collective-permute-done | bytes 131104 | tf_op jit(solution)/shard_map/ppermute | solution.py:507
  68.6 3.0 %collective-permute-start.14 = (bf16[512,128]{1,0:T(8,128)(2,1)S(1)}, bf16[512,128]{1,0:T(8,128)(2,1)S(1)}, u32[]{:S(2)}, u32[]{:S(2)}) collective-permute-start(bf16[512,128]{1,0:T(8,128)(2,1)S(1)} %copy-done.3), channel_id=1, source_target_pairs={{0,1},{1,0},{2,3},{3,2},{4,5},{5,4},{6,7},{7,6},{8,9},{9,8},{10,11... | collective-permute-start | bytes 393224 | tf_op jit(solution)/shard_map/ppermute | solution.py:507
  71.7 1.4 collective-permute-done.10.refs_10_
  73.3 1.2 collective-permute-start.34
  74.5 2.0 %collective-permute-start.33 = (bf16[4,256,128]{2,1,0:T(8,128)(2,1)S(1)}, bf16[4,256,128]{2,1,0:T(8,128)(2,1)S(1)}, u32[]{:S(2)}, u32[]{:S(2)}) collective-permute-start(bf16[4,256,128]{2,1,0:T(8,128)(2,1)S(1)} %pad_maximum_fusion), channel_id=1, source_target_pairs={{0,1},{1,0},{2,3},{3,2},{4,5},{5,4},{6,7},{7,6},{8,9},{9,8},{10,11... | collective-permute-start | bytes 786440 | tf_op jit(solution)/shard_map/ppermute | solution.py:507
  76.5 16.6 %whole_head.1 = (bf16[528,128]{1,0:T(8,128)(2,1)S(1)}, bf16[528,128]{1,0:T(8,128)(2,1)S(1)}, bf16[528,128]{1,0:T(8,128)(2,1)S(1)}, bf16[528,128]{1,0:T(8,128)(2,...) custom-call(s32[1]{0:T(128)} %bitcast.place_ref, ...), custom_call_target="tpu_custom_call" | custom-call | flops 3321888768 | bytes 4194304 | tf_op jit(solution)/shard_map/whole_head/pallas_call | solution.py:550
  93.2 2.1 %collective-permute-start.15 = (bf16[528,128]{1,0:T(8,128)(2,1)}, bf16[528,128]{1,0:T(8,128)(2,1)S(1)}, u32[]{:S(2)}, u32[]{:S(2)}) collective-permute-start(bf16[528,128]{1,0:T(8,128)(2,1)} %get-tuple-element.67), channel_id=1, source_target_pairs={{0,15},{1,14},{2,13},{3,12},{4,11},{5,10},{6,9},{7,8},{8,7},{9,6},... | collective-permute-start | bytes 405512 | tf_op jit(solution)/shard_map/ppermute | solution.py:507
  95.2 2.0 %collective-permute-start.16 = (bf16[528,128]{1,0:T(8,128)(2,1)}, bf16[528,128]{1,0:T(8,128)(2,1)S(1)}, u32[]{:S(2)}, u32[]{:S(2)}) collective-permute-start(bf16[528,128]{1,0:T(8,128)(2,1)} %get-tuple-element.68), channel_id=1, source_target_pairs={{0,14},{1,15},{2,12},{3,13},{4,10},{5,11},{6,8},{7,9},{8,6},{9,7},... | collective-permute-start | bytes 405512 | tf_op jit(solution)/shard_map/ppermute | solution.py:507
  97.2 2.9 %collective-permute-start.17 = (bf16[528,128]{1,0:T(8,128)(2,1)S(1)}, bf16[528,128]{1,0:T(8,128)(2,1)S(1)}, u32[]{:S(2)}, u32[]{:S(2)}) collective-permute-start(bf16[528,128]{1,0:T(8,128)(2,1)S(1)} %get-tuple-element.69), channel_id=1, source_target_pairs={{0,13},{1,12},{2,15},{3,14},{4,9},{5,8},{6,11},{7,10},{8,5},{9,4},... | collective-permute-start | bytes 405512 | tf_op jit(solution)/shard_map/ppermute | solution.py:507
  100.1 1.1 collective-permute-start.18
  101.2 6.1 %shared_head.1 = (bf16[4,256,128]{2,1,0:T(8,128)(2,1)S(1)}, f32[4,264,128]{2,1,0:T(8,128)S(1)}, bf16[4,272,128]{2,1,0:T(8,128)(2,1)S(1)}, bf16[4,272,128]{2,1,0:T(8,128)(2,1)S(1)}, bf16[4,272,128]{2,1,0:T(8,128)(2,1)S(1)}) custom-call(s32[1]{0:T(128)} %bitcast.place_ref, s32[16,8]{1,0:T(8,128)S(1)} %copy.11.sel_ref, bf16[512,128]{1,0:T(8,128)(2,1)S(1)} %copy-done, ...), custom_call_target="tpu_custom_call" | custom-call | flops 830472192 | bytes 4194304 | tf_op jit(solution)/shard_map/shared_head/pallas_call | solution.py:525
  107.4 0.3 collective-permute-start.37
  107.7 1.8 %collective-permute-start.38 = (bf16[4,272,128]{2,1,0:T(8,128)(2,1)S(1)}, bf16[4,272,128]{2,1,0:T(8,128)(2,1)S(1)}, u32[]{:S(2)}, u32[]{:S(2)}) collective-permute-start(bf16[4,272,128]{2,1,0:T(8,128)(2,1)S(1)} %get-tuple-element.91), channel_id=1, source_target_pairs={{0,3},{1,2},{2,1},{3,0},{4,7},{5,6},{6,5},{7,4},{8,11},{9,10},{10,... | collective-permute-start | bytes 835592 | tf_op jit(solution)/shard_map/ppermute | solution.py:507
  109.5 7.6 %collective-permute-start.19 = (bf16[528,128]{1,0:T(8,128)(2,1)S(1)}, bf16[528,128]{1,0:T(8,128)(2,1)S(1)}, u32[]{:S(2)}, u32[]{:S(2)}) collective-permute-start(bf16[528,128]{1,0:T(8,128)(2,1)S(1)} %get-tuple-element.71), channel_id=1, source_target_pairs={{0,11},{1,10},{2,9},{3,8},{4,15},{5,14},{6,13},{7,12},{8,3},{9,2},... | collective-permute-start | bytes 405512 | tf_op jit(solution)/shard_map/ppermute | solution.py:507
  117.2 2.6 %collective-permute-start.20 = (bf16[528,128]{1,0:T(8,128)(2,1)S(1)}, bf16[528,128]{1,0:T(8,128)(2,1)S(1)}, u32[]{:S(2)}, u32[]{:S(2)}) collective-permute-start(bf16[528,128]{1,0:T(8,128)(2,1)S(1)} %get-tuple-element.72), channel_id=1, source_target_pairs={{0,10},{1,11},{2,8},{3,9},{4,14},{5,15},{6,12},{7,13},{8,2},{9,3},... | collective-permute-start | bytes 405512 | tf_op jit(solution)/shard_map/ppermute | solution.py:507
  119.8 7.8 %collective-permute-done.19.refs_4_ = bf16[528,128]{1,0:T(8,128)(2,1)S(1)} collective-permute-done((bf16[528,128]{1,0:T(8,128)(2,1)S(1)}, bf16[528,128]{1,0:T(8,128)(2,1)S(1)}, u32[]{:S(2)}, u32[]{:S(2)}) %collective-permute-start.19) | collective-permute-done | bytes 135200 | tf_op jit(solution)/shard_map/ppermute | solution.py:507
  127.5 7.4 %collective-permute-done.20.refs_5_ = bf16[528,128]{1,0:T(8,128)(2,1)S(1)} collective-permute-done((bf16[528,128]{1,0:T(8,128)(2,1)S(1)}, bf16[528,128]{1,0:T(8,128)(2,1)S(1)}, u32[]{:S(2)}, u32[]{:S(2)}) %collective-permute-start.20) | collective-permute-done | bytes 135200 | tf_op jit(solution)/shard_map/ppermute | solution.py:507
  135.0 3.4 %collective-permute-done.21.refs_6_ = bf16[528,128]{1,0:T(8,128)(2,1)S(1)} collective-permute-done((bf16[528,128]{1,0:T(8,128)(2,1)S(1)}, bf16[528,128]{1,0:T(8,128)(2,1)S(1)}, u32[]{:S(2)}, u32[]{:S(2)}) %collective-permute-start.21) | collective-permute-done | bytes 135200 | tf_op jit(solution)/shard_map/ppermute | solution.py:507
  138.4 1.4 collective-permute-start.23
  139.7 3.1 %collective-permute-done.22.refs_7_ = bf16[528,128]{1,0:T(8,128)(2,1)S(1)} collective-permute-done((bf16[528,128]{1,0:T(8,128)(2,1)S(1)}, bf16[528,128]{1,0:T(8,128)(2,1)S(1)}, u32[]{:S(2)}, u32[]{:S(2)}) %collective-permute-start.22) | collective-permute-done | bytes 135200 | tf_op jit(solution)/shard_map/ppermute | solution.py:507
  142.8 1.3 collective-permute-start.25
  144.2 0.3 collective-permute-start.26
  144.5 1.8 %collective-permute-start.27 = (bf16[528,128]{1,0:T(8,128)(2,1)S(1)}, bf16[528,128]{1,0:T(8,128)(2,1)S(1)}, u32[]{:S(2)}, u32[]{:S(2)}) collective-permute-start(bf16[528,128]{1,0:T(8,128)(2,1)S(1)} %get-tuple-element.79), channel_id=1, source_target_pairs={{0,3},{1,2},{2,1},{3,0},{4,7},{5,6},{6,5},{7,4},{8,11},{9,10},{10,... | collective-permute-start | bytes 405512 | tf_op jit(solution)/shard_map/ppermute | solution.py:507
  146.5 2.0 %collective-permute-done.24.refs_9_ = bf16[528,128]{1,0:T(8,128)(2,1)S(1)} collective-permute-done((bf16[528,128]{1,0:T(8,128)(2,1)S(1)}, bf16[528,128]{1,0:T(8,128)(2,1)S(1)}, u32[]{:S(2)}, u32[]{:S(2)}) %collective-permute-start.24) | collective-permute-done | bytes 135200 | tf_op jit(solution)/shard_map/ppermute | solution.py:507
  148.6 1.9 %collective-permute-start.29 = (bf16[528,128]{1,0:T(8,128)(2,1)S(1)}, bf16[528,128]{1,0:T(8,128)(2,1)S(1)}, u32[]{:S(2)}, u32[]{:S(2)}) collective-permute-start(bf16[528,128]{1,0:T(8,128)(2,1)S(1)} %get-tuple-element.81), channel_id=1, source_target_pairs={{0,1},{1,0},{2,3},{3,2},{4,5},{5,4},{6,7},{7,6},{8,9},{9,8},{10,11... | collective-permute-start | bytes 405512 | tf_op jit(solution)/shard_map/ppermute | solution.py:507
  150.4 1.0 collective-permute-done.25.refs_10_
  151.5 2.5 %collective-permute-start.39 = (bf16[528,128]{1,0:T(8,128)(2,1)S(1)}, bf16[528,128]{1,0:T(8,128)(2,1)S(1)}, u32[]{:S(2)}, u32[]{:S(2)}) collective-permute-start(bf16[528,128]{1,0:T(8,128)(2,1)S(1)} %get-tuple-element.92), channel_id=1, source_target_pairs={{0,12},{1,13},{2,14},{3,15},{4,8},{5,9},{6,10},{7,11},{8,4},{9,5},... | collective-permute-start | bytes 405512 | tf_op jit(solution)/shard_map/ppermute | solution.py:507
  154.0 1.1 collective-permute-start.41
  155.1 3.6 %collective-permute-done.39.refs_16_ = bf16[528,128]{1,0:T(8,128)(2,1)S(1)} collective-permute-done((bf16[528,128]{1,0:T(8,128)(2,1)S(1)}, bf16[528,128]{1,0:T(8,128)(2,1)S(1)}, u32[]{:S(2)}, u32[]{:S(2)}) %collective-permute-start.39) | collective-permute-done | bytes 135200 | tf_op jit(solution)/shard_map/ppermute | solution.py:507
  158.6 6.6 %collective-permute-done.40.refs_17_ = bf16[528,128]{1,0:T(8,128)(2,1)S(1)} collective-permute-done((bf16[528,128]{1,0:T(8,128)(2,1)S(1)}, bf16[528,128]{1,0:T(8,128)(2,1)S(1)}, u32[]{:S(2)}, u32[]{:S(2)}) %collective-permute-start.40) | collective-permute-done | bytes 135200 | tf_op jit(solution)/shard_map/ppermute | solution.py:507
  165.3 2.0 %unpack.1 = (bf16[128,2560]{1,0:T(8,128)(2,1)}, bf16[128,2560]{1,0:T(8,128)(2,1)}, bf16[128,2560]{1,0:T(8,128)(2,1)}, bf16[128,2560]{1,0:T(8,128)(2,1)}, f32[2,2560]{1,0:T(2,128)}, /*index=5*/f32[2,2560]{1,0:T(2,128)}) custom-call(s32[1]{0:T(128)} %bitcast.place_ref, bf16[528,128]{1,0:T(8,128)(2,1)S(1)} %collective-permute-done.15.refs_0_, ...), custom_call_target="tpu_custom_call" | custom-call | tf_op jit(solution)/shard_map/unpack/pallas_call | solution.py:567
  (60 shorter events, 1.6 us)
Async XLA Ops:
  2.6 13.5 %collective-permute-start.30 = (bf16[512,128]{1,0:T(8,128)(2,1)}, bf16[512,128]{1,0:T(8,128)(2,1)S(1)}, u32[]{:S(2)}, u32[]{:S(2)}) collective-permute-start(bf16[512,128]{1,0:T(8,128)(2,1)} %get-tuple-element.84), channel_id=1, source_target_pairs={{0,4},{1,5},{2,6},{3,7},{4,0},{5,1},{6,2},{7,3},{8,12},{9,13},{10,... | collective-permute-start | bytes 393224 | tf_op jit(solution)/shard_map/ppermute | solution.py:507
  4.8 13.9 %collective-permute-start.31 = (bf16[512,128]{1,0:T(8,128)(2,1)}, bf16[512,128]{1,0:T(8,128)(2,1)S(1)}, u32[]{:S(2)}, u32[]{:S(2)}) collective-permute-start(bf16[512,128]{1,0:T(8,128)(2,1)} %get-tuple-element.85), channel_id=1, source_target_pairs={{0,8},{1,9},{2,10},{3,11},{4,12},{5,13},{6,14},{7,15},{8,0},{9,1},... | collective-permute-start | bytes 393224 | tf_op jit(solution)/shard_map/ppermute | solution.py:507
  7.1 9.1 %copy-start = (bf16[512,128]{1,0:T(8,128)(2,1)S(1)}, bf16[512,128]{1,0:T(8,128)(2,1)}, u32[]{:S(2)}) copy-start(bf16[512,128]{1,0:T(8,128)(2,1)} %get-tuple-element.83.refs_0_) | copy-start | bytes 393220
  7.1 12.8 %collective-permute-start.32 = (bf16[512,128]{1,0:T(8,128)(2,1)}, bf16[512,128]{1,0:T(8,128)(2,1)S(1)}, u32[]{:S(2)}, u32[]{:S(2)}) collective-permute-start(bf16[512,128]{1,0:T(8,128)(2,1)} %get-tuple-element.86), channel_id=1, source_target_pairs={{0,12},{1,13},{2,14},{3,15},{4,8},{5,9},{6,10},{7,11},{8,4},{9,5},... | collective-permute-start | bytes 393224 | tf_op jit(solution)/shard_map/ppermute | solution.py:507
  7.1 9.0 %copy-start.2 = (s32[16,8]{0,1:T(8,128)S(1)}, s32[16,8]{0,1:T(8,128)}, u32[]{:S(2)}) copy-start(s32[16,8]{0,1:T(8,128)} %param.9) | copy-start | bytes 1540
  10.5 22.9 %collective-permute-start = (bf16[512,128]{1,0:T(8,128)(2,1)}, bf16[512,128]{1,0:T(8,128)(2,1)S(1)}, u32[]{:S(2)}, u32[]{:S(2)}) collective-permute-start(bf16[512,128]{1,0:T(8,128)(2,1)} %get-tuple-element.51), channel_id=1, source_target_pairs={{0,15},{1,14},{2,13},{3,12},{4,11},{5,10},{6,9},{7,8},{8,7},{9,6},... | collective-permute-start | bytes 393224 | tf_op jit(solution)/shard_map/ppermute | solution.py:507
  16.1 19.5 %collective-permute-start.1 = (bf16[512,128]{1,0:T(8,128)(2,1)}, bf16[512,128]{1,0:T(8,128)(2,1)S(1)}, u32[]{:S(2)}, u32[]{:S(2)}) collective-permute-start(bf16[512,128]{1,0:T(8,128)(2,1)} %get-tuple-element.52), channel_id=1, source_target_pairs={{0,14},{1,15},{2,12},{3,13},{4,10},{5,11},{6,8},{7,9},{8,6},{9,7},... | collective-permute-start | bytes 393224 | tf_op jit(solution)/shard_map/ppermute | solution.py:507
  16.2 47.3 %copy-start.5 = (bf16[512,128]{1,0:T(8,128)(2,1)S(1)}, bf16[512,128]{1,0:T(8,128)(2,1)}, u32[]{:S(2)}) copy-start(bf16[512,128]{1,0:T(8,128)(2,1)} %get-tuple-element.63) | copy-start | bytes 393220
  16.2 29.8 %collective-permute-start.2 = (bf16[512,128]{1,0:T(8,128)(2,1)}, bf16[512,128]{1,0:T(8,128)(2,1)S(1)}, u32[]{:S(2)}, u32[]{:S(2)}) collective-permute-start(bf16[512,128]{1,0:T(8,128)(2,1)} %get-tuple-element.53), channel_id=1, source_target_pairs={{0,13},{1,12},{2,15},{3,14},{4,9},{5,8},{6,11},{7,10},{8,5},{9,4},... | collective-permute-start | bytes 393224 | tf_op jit(solution)/shard_map/ppermute | solution.py:507
  18.6 28.7 %collective-permute-start.3 = (bf16[512,128]{1,0:T(8,128)(2,1)}, bf16[512,128]{1,0:T(8,128)(2,1)S(1)}, u32[]{:S(2)}, u32[]{:S(2)}) collective-permute-start(bf16[512,128]{1,0:T(8,128)(2,1)} %get-tuple-element.54), channel_id=1, source_target_pairs={{0,12},{1,13},{2,14},{3,15},{4,8},{5,9},{6,10},{7,11},{8,4},{9,5},... | collective-permute-start | bytes 393224 | tf_op jit(solution)/shard_map/ppermute | solution.py:507
  19.9 48.3 %copy-start.4 = (bf16[512,128]{1,0:T(8,128)(2,1)S(1)}, bf16[512,128]{1,0:T(8,128)(2,1)}, u32[]{:S(2)}) copy-start(bf16[512,128]{1,0:T(8,128)(2,1)} %get-tuple-element.64) | copy-start | bytes 393220
  19.9 48.8 %copy-start.3 = (bf16[512,128]{1,0:T(8,128)(2,1)S(1)}, bf16[512,128]{1,0:T(8,128)(2,1)}, u32[]{:S(2)}) copy-start(bf16[512,128]{1,0:T(8,128)(2,1)} %get-tuple-element.65) | copy-start | bytes 393220
  19.9 38.6 %collective-permute-start.4 = (bf16[512,128]{1,0:T(8,128)(2,1)}, bf16[512,128]{1,0:T(8,128)(2,1)S(1)}, u32[]{:S(2)}, u32[]{:S(2)}) collective-permute-start(bf16[512,128]{1,0:T(8,128)(2,1)} %get-tuple-element.55), channel_id=1, source_target_pairs={{0,11},{1,10},{2,9},{3,8},{4,15},{5,14},{6,13},{7,12},{8,3},{9,2},... | collective-permute-start | bytes 393224 | tf_op jit(solution)/shard_map/ppermute | solution.py:507
  33.4 25.4 %collective-permute-start.5 = (bf16[512,128]{1,0:T(8,128)(2,1)}, bf16[512,128]{1,0:T(8,128)(2,1)S(1)}, u32[]{:S(2)}, u32[]{:S(2)}) collective-permute-start(bf16[512,128]{1,0:T(8,128)(2,1)} %get-tuple-element.56), channel_id=1, source_target_pairs={{0,10},{1,11},{2,8},{3,9},{4,14},{5,15},{6,12},{7,13},{8,2},{9,3},... | collective-permute-start | bytes 393224 | tf_op jit(solution)/shard_map/ppermute | solution.py:507
  35.6 27.6 %collective-permute-start.6 = (bf16[512,128]{1,0:T(8,128)(2,1)}, bf16[512,128]{1,0:T(8,128)(2,1)S(1)}, u32[]{:S(2)}, u32[]{:S(2)}) collective-permute-start(bf16[512,128]{1,0:T(8,128)(2,1)} %get-tuple-element.57), channel_id=1, source_target_pairs={{0,9},{1,8},{2,11},{3,10},{4,13},{5,12},{6,15},{7,14},{8,1},{9,0},... | collective-permute-start | bytes 393224 | tf_op jit(solution)/shard_map/ppermute | solution.py:507
  46.0 17.5 %collective-permute-start.7 = (bf16[512,128]{1,0:T(8,128)(2,1)}, bf16[512,128]{1,0:T(8,128)(2,1)S(1)}, u32[]{:S(2)}, u32[]{:S(2)}) collective-permute-start(bf16[512,128]{1,0:T(8,128)(2,1)} %get-tuple-element.58), channel_id=1, source_target_pairs={{0,8},{1,9},{2,10},{3,11},{4,12},{5,13},{6,14},{7,15},{8,0},{9,1},... | collective-permute-start | bytes 393224 | tf_op jit(solution)/shard_map/ppermute | solution.py:507
  47.3 20.9 %collective-permute-start.8 = (bf16[512,128]{1,0:T(8,128)(2,1)}, bf16[512,128]{1,0:T(8,128)(2,1)S(1)}, u32[]{:S(2)}, u32[]{:S(2)}) collective-permute-start(bf16[512,128]{1,0:T(8,128)(2,1)} %get-tuple-element.59), channel_id=1, source_target_pairs={{0,7},{1,6},{2,5},{3,4},{4,3},{5,2},{6,1},{7,0},{8,15},{9,14},{10,... | collective-permute-start | bytes 393224 | tf_op jit(solution)/shard_map/ppermute | solution.py:507
  58.5 10.2 %collective-permute-start.9 = (bf16[512,128]{1,0:T(8,128)(2,1)}, bf16[512,128]{1,0:T(8,128)(2,1)S(1)}, u32[]{:S(2)}, u32[]{:S(2)}) collective-permute-start(bf16[512,128]{1,0:T(8,128)(2,1)} %get-tuple-element.60), channel_id=1, source_target_pairs={{0,6},{1,7},{2,4},{3,5},{4,2},{5,3},{6,0},{7,1},{8,14},{9,15},{10,... | collective-permute-start | bytes 393224 | tf_op jit(solution)/shard_map/ppermute | solution.py:507
  58.7 14.4 %collective-permute-start.10 = (bf16[512,128]{1,0:T(8,128)(2,1)}, bf16[512,128]{1,0:T(8,128)(2,1)S(1)}, u32[]{:S(2)}, u32[]{:S(2)}) collective-permute-start(bf16[512,128]{1,0:T(8,128)(2,1)} %get-tuple-element.61), channel_id=1, source_target_pairs={{0,5},{1,4},{2,7},{3,6},{4,1},{5,0},{6,3},{7,2},{8,13},{9,12},{10,... | collective-permute-start | bytes 393224 | tf_op jit(solution)/shard_map/ppermute | solution.py:507
  63.2 10.2 %collective-permute-start.11 = (bf16[512,128]{1,0:T(8,128)(2,1)}, bf16[512,128]{1,0:T(8,128)(2,1)S(1)}, u32[]{:S(2)}, u32[]{:S(2)}) collective-permute-start(bf16[512,128]{1,0:T(8,128)(2,1)} %get-tuple-element.62), channel_id=1, source_target_pairs={{0,4},{1,5},{2,6},{3,7},{4,0},{5,1},{6,2},{7,3},{8,12},{9,13},{10,... | collective-permute-start | bytes 393224 | tf_op jit(solution)/shard_map/ppermute | solution.py:507
  63.5 11.1 %collective-permute-start.12 = (bf16[512,128]{1,0:T(8,128)(2,1)S(1)}, bf16[512,128]{1,0:T(8,128)(2,1)S(1)}, u32[]{:S(2)}, u32[]{:S(2)}) collective-permute-start(bf16[512,128]{1,0:T(8,128)(2,1)S(1)} %copy-done.5), channel_id=1, source_target_pairs={{0,3},{1,2},{2,1},{3,0},{4,7},{5,6},{6,5},{7,4},{8,11},{9,10},{10,... | collective-permute-start | bytes 393224 | tf_op jit(solution)/shard_map/ppermute | solution.py:507
  68.2 8.3 %collective-permute-start.13 = (bf16[512,128]{1,0:T(8,128)(2,1)S(1)}, bf16[512,128]{1,0:T(8,128)(2,1)S(1)}, u32[]{:S(2)}, u32[]{:S(2)}) collective-permute-start(bf16[512,128]{1,0:T(8,128)(2,1)S(1)} %copy-done.4), channel_id=1, source_target_pairs={{0,2},{1,3},{2,0},{3,1},{4,6},{5,7},{6,4},{7,5},{8,10},{9,11},{10,... | collective-permute-start | bytes 393224 | tf_op jit(solution)/shard_map/ppermute | solution.py:507
  68.6 7.9 %collective-permute-start.14 = (bf16[512,128]{1,0:T(8,128)(2,1)S(1)}, bf16[512,128]{1,0:T(8,128)(2,1)S(1)}, u32[]{:S(2)}, u32[]{:S(2)}) collective-permute-start(bf16[512,128]{1,0:T(8,128)(2,1)S(1)} %copy-done.3), channel_id=1, source_target_pairs={{0,1},{1,0},{2,3},{3,2},{4,5},{5,4},{6,7},{7,6},{8,9},{9,8},{10,11... | collective-permute-start | bytes 393224 | tf_op jit(solution)/shard_map/ppermute | solution.py:507
  71.7 4.9 %copy-start.1 = (bf16[512,128]{1,0:T(8,128)(2,1)S(1)}, bf16[512,128]{1,0:T(8,128)(2,1)}, u32[]{:S(2)}) copy-start(bf16[512,128]{1,0:T(8,128)(2,1)} %get-tuple-element.66.refs_15_) | copy-start | bytes 393220
  73.1 24.1 %collective-permute-start.35 = (bf16[4,256,128]{2,1,0:T(8,128)(2,1)S(1)}, bf16[4,256,128]{2,1,0:T(8,128)(2,1)S(1)}, u32[]{:S(2)}, u32[]{:S(2)}) collective-permute-start(bf16[4,256,128]{2,1,0:T(8,128)(2,1)S(1)} %pad_maximum_fusion), channel_id=1, source_target_pairs={{0,3},{1,2},{2,1},{3,0},{4,7},{5,6},{6,5},{7,4},{8,11},{9,10},{10,... | collective-permute-start | bytes 786440 | tf_op jit(solution)/shard_map/ppermute | solution.py:507
  73.3 26.8 %collective-permute-start.34 = (bf16[4,256,128]{2,1,0:T(8,128)(2,1)S(1)}, bf16[4,256,128]{2,1,0:T(8,128)(2,1)S(1)}, u32[]{:S(2)}, u32[]{:S(2)}) collective-permute-start(bf16[4,256,128]{2,1,0:T(8,128)(2,1)S(1)} %pad_maximum_fusion), channel_id=1, source_target_pairs={{0,2},{1,3},{2,0},{3,1},{4,6},{5,7},{6,4},{7,5},{8,10},{9,11},{10,... | collective-permute-start | bytes 786440 | tf_op jit(solution)/shard_map/ppermute | solution.py:507
  74.5 26.6 %collective-permute-start.33 = (bf16[4,256,128]{2,1,0:T(8,128)(2,1)S(1)}, bf16[4,256,128]{2,1,0:T(8,128)(2,1)S(1)}, u32[]{:S(2)}, u32[]{:S(2)}) collective-permute-start(bf16[4,256,128]{2,1,0:T(8,128)(2,1)S(1)} %pad_maximum_fusion), channel_id=1, source_target_pairs={{0,1},{1,0},{2,3},{3,2},{4,5},{5,4},{6,7},{7,6},{8,9},{9,8},{10,11... | collective-permute-start | bytes 786440 | tf_op jit(solution)/shard_map/ppermute | solution.py:507
  93.2 14.2 %collective-permute-start.15 = (bf16[528,128]{1,0:T(8,128)(2,1)}, bf16[528,128]{1,0:T(8,128)(2,1)S(1)}, u32[]{:S(2)}, u32[]{:S(2)}) collective-permute-start(bf16[528,128]{1,0:T(8,128)(2,1)} %get-tuple-element.67), channel_id=1, source_target_pairs={{0,15},{1,14},{2,13},{3,12},{4,11},{5,10},{6,9},{7,8},{8,7},{9,6},... | collective-permute-start | bytes 405512 | tf_op jit(solution)/shard_map/ppermute | solution.py:507
  95.2 12.5 %collective-permute-start.16 = (bf16[528,128]{1,0:T(8,128)(2,1)}, bf16[528,128]{1,0:T(8,128)(2,1)S(1)}, u32[]{:S(2)}, u32[]{:S(2)}) collective-permute-start(bf16[528,128]{1,0:T(8,128)(2,1)} %get-tuple-element.68), channel_id=1, source_target_pairs={{0,14},{1,15},{2,12},{3,13},{4,10},{5,11},{6,8},{7,9},{8,6},{9,7},... | collective-permute-start | bytes 405512 | tf_op jit(solution)/shard_map/ppermute | solution.py:507
  97.2 12.3 %collective-permute-start.17 = (bf16[528,128]{1,0:T(8,128)(2,1)S(1)}, bf16[528,128]{1,0:T(8,128)(2,1)S(1)}, u32[]{:S(2)}, u32[]{:S(2)}) collective-permute-start(bf16[528,128]{1,0:T(8,128)(2,1)S(1)} %get-tuple-element.69), channel_id=1, source_target_pairs={{0,13},{1,12},{2,15},{3,14},{4,9},{5,8},{6,11},{7,10},{8,5},{9,4},... | collective-permute-start | bytes 405512 | tf_op jit(solution)/shard_map/ppermute | solution.py:507
  100.1 17.1 %collective-permute-start.18 = (bf16[528,128]{1,0:T(8,128)(2,1)S(1)}, bf16[528,128]{1,0:T(8,128)(2,1)S(1)}, u32[]{:S(2)}, u32[]{:S(2)}) collective-permute-start(bf16[528,128]{1,0:T(8,128)(2,1)S(1)} %get-tuple-element.70), channel_id=1, source_target_pairs={{0,12},{1,13},{2,14},{3,15},{4,8},{5,9},{6,10},{7,11},{8,4},{9,5},... | collective-permute-start | bytes 405512 | tf_op jit(solution)/shard_map/ppermute | solution.py:507
  107.3 35.5 %collective-permute-start.36 = (bf16[4,272,128]{2,1,0:T(8,128)(2,1)S(1)}, bf16[4,272,128]{2,1,0:T(8,128)(2,1)S(1)}, u32[]{:S(2)}, u32[]{:S(2)}) collective-permute-start(bf16[4,272,128]{2,1,0:T(8,128)(2,1)S(1)} %get-tuple-element.89), channel_id=1, source_target_pairs={{0,1},{1,0},{2,3},{3,2},{4,5},{5,4},{6,7},{7,6},{8,9},{9,8},{10,11... | collective-permute-start | bytes 835592 | tf_op jit(solution)/shard_map/ppermute | solution.py:507
  107.4 36.8 %collective-permute-start.37 = (bf16[4,272,128]{2,1,0:T(8,128)(2,1)S(1)}, bf16[4,272,128]{2,1,0:T(8,128)(2,1)S(1)}, u32[]{:S(2)}, u32[]{:S(2)}) collective-permute-start(bf16[4,272,128]{2,1,0:T(8,128)(2,1)S(1)} %get-tuple-element.90), channel_id=1, source_target_pairs={{0,2},{1,3},{2,0},{3,1},{4,6},{5,7},{6,4},{7,5},{8,10},{9,11},{10,... | collective-permute-start | bytes 835592 | tf_op jit(solution)/shard_map/ppermute | solution.py:507
  107.7 36.7 %collective-permute-start.38 = (bf16[4,272,128]{2,1,0:T(8,128)(2,1)S(1)}, bf16[4,272,128]{2,1,0:T(8,128)(2,1)S(1)}, u32[]{:S(2)}, u32[]{:S(2)}) collective-permute-start(bf16[4,272,128]{2,1,0:T(8,128)(2,1)S(1)} %get-tuple-element.91), channel_id=1, source_target_pairs={{0,3},{1,2},{2,1},{3,0},{4,7},{5,6},{6,5},{7,4},{8,11},{9,10},{10,... | collective-permute-start | bytes 835592 | tf_op jit(solution)/shard_map/ppermute | solution.py:507
  109.5 18.0 %collective-permute-start.19 = (bf16[528,128]{1,0:T(8,128)(2,1)S(1)}, bf16[528,128]{1,0:T(8,128)(2,1)S(1)}, u32[]{:S(2)}, u32[]{:S(2)}) collective-permute-start(bf16[528,128]{1,0:T(8,128)(2,1)S(1)} %get-tuple-element.71), channel_id=1, source_target_pairs={{0,11},{1,10},{2,9},{3,8},{4,15},{5,14},{6,13},{7,12},{8,3},{9,2},... | collective-permute-start | bytes 405512 | tf_op jit(solution)/shard_map/ppermute | solution.py:507
  117.2 17.8 %collective-permute-start.20 = (bf16[528,128]{1,0:T(8,128)(2,1)S(1)}, bf16[528,128]{1,0:T(8,128)(2,1)S(1)}, u32[]{:S(2)}, u32[]{:S(2)}) collective-permute-start(bf16[528,128]{1,0:T(8,128)(2,1)S(1)} %get-tuple-element.72), channel_id=1, source_target_pairs={{0,10},{1,11},{2,8},{3,9},{4,14},{5,15},{6,12},{7,13},{8,2},{9,3},... | collective-permute-start | bytes 405512 | tf_op jit(solution)/shard_map/ppermute | solution.py:507
  127.5 10.9 %collective-permute-start.21 = (bf16[528,128]{1,0:T(8,128)(2,1)S(1)}, bf16[528,128]{1,0:T(8,128)(2,1)S(1)}, u32[]{:S(2)}, u32[]{:S(2)}) collective-permute-start(bf16[528,128]{1,0:T(8,128)(2,1)S(1)} %get-tuple-element.73), channel_id=1, source_target_pairs={{0,9},{1,8},{2,11},{3,10},{4,13},{5,12},{6,15},{7,14},{8,1},{9,0},... | collective-permute-start | bytes 405512 | tf_op jit(solution)/shard_map/ppermute | solution.py:507
  135.0 7.8 %collective-permute-start.22 = (bf16[528,128]{1,0:T(8,128)(2,1)S(1)}, bf16[528,128]{1,0:T(8,128)(2,1)S(1)}, u32[]{:S(2)}, u32[]{:S(2)}) collective-permute-start(bf16[528,128]{1,0:T(8,128)(2,1)S(1)} %get-tuple-element.74), channel_id=1, source_target_pairs={{0,8},{1,9},{2,10},{3,11},{4,12},{5,13},{6,14},{7,15},{8,0},{9,1},... | collective-permute-start | bytes 405512 | tf_op jit(solution)/shard_map/ppermute | solution.py:507
  138.4 8.0 %collective-permute-start.23 = (bf16[528,128]{1,0:T(8,128)(2,1)S(1)}, bf16[528,128]{1,0:T(8,128)(2,1)S(1)}, u32[]{:S(2)}, u32[]{:S(2)}) collective-permute-start(bf16[528,128]{1,0:T(8,128)(2,1)S(1)} %get-tuple-element.75), channel_id=1, source_target_pairs={{0,7},{1,6},{2,5},{3,4},{4,3},{5,2},{6,1},{7,0},{8,15},{9,14},{10,... | collective-permute-start | bytes 405512 | tf_op jit(solution)/shard_map/ppermute | solution.py:507
  142.8 5.8 %collective-permute-start.24 = (bf16[528,128]{1,0:T(8,128)(2,1)S(1)}, bf16[528,128]{1,0:T(8,128)(2,1)S(1)}, u32[]{:S(2)}, u32[]{:S(2)}) collective-permute-start(bf16[528,128]{1,0:T(8,128)(2,1)S(1)} %get-tuple-element.76), channel_id=1, source_target_pairs={{0,6},{1,7},{2,4},{3,5},{4,2},{5,3},{6,0},{7,1},{8,14},{9,15},{10,... | collective-permute-start | bytes 405512 | tf_op jit(solution)/shard_map/ppermute | solution.py:507
  142.8 8.7 %collective-permute-start.25 = (bf16[528,128]{1,0:T(8,128)(2,1)S(1)}, bf16[528,128]{1,0:T(8,128)(2,1)S(1)}, u32[]{:S(2)}, u32[]{:S(2)}) collective-permute-start(bf16[528,128]{1,0:T(8,128)(2,1)S(1)} %get-tuple-element.77), channel_id=1, source_target_pairs={{0,5},{1,4},{2,7},{3,6},{4,1},{5,0},{6,3},{7,2},{8,13},{9,12},{10,... | collective-permute-start | bytes 405512 | tf_op jit(solution)/shard_map/ppermute | solution.py:507
  144.2 9.8 %collective-permute-start.26 = (bf16[528,128]{1,0:T(8,128)(2,1)S(1)}, bf16[528,128]{1,0:T(8,128)(2,1)S(1)}, u32[]{:S(2)}, u32[]{:S(2)}) collective-permute-start(bf16[528,128]{1,0:T(8,128)(2,1)S(1)} %get-tuple-element.78), channel_id=1, source_target_pairs={{0,4},{1,5},{2,6},{3,7},{4,0},{5,1},{6,2},{7,3},{8,12},{9,13},{10,... | collective-permute-start | bytes 405512 | tf_op jit(solution)/shard_map/ppermute | solution.py:507
  144.5 9.5 %collective-permute-start.27 = (bf16[528,128]{1,0:T(8,128)(2,1)S(1)}, bf16[528,128]{1,0:T(8,128)(2,1)S(1)}, u32[]{:S(2)}, u32[]{:S(2)}) collective-permute-start(bf16[528,128]{1,0:T(8,128)(2,1)S(1)} %get-tuple-element.79), channel_id=1, source_target_pairs={{0,3},{1,2},{2,1},{3,0},{4,7},{5,6},{6,5},{7,4},{8,11},{9,10},{10,... | collective-permute-start | bytes 405512 | tf_op jit(solution)/shard_map/ppermute | solution.py:507
  146.4 8.7 %collective-permute-start.28 = (bf16[528,128]{1,0:T(8,128)(2,1)S(1)}, bf16[528,128]{1,0:T(8,128)(2,1)S(1)}, u32[]{:S(2)}, u32[]{:S(2)}) collective-permute-start(bf16[528,128]{1,0:T(8,128)(2,1)S(1)} %get-tuple-element.80), channel_id=1, source_target_pairs={{0,2},{1,3},{2,0},{3,1},{4,6},{5,7},{6,4},{7,5},{8,10},{9,11},{10,... | collective-permute-start | bytes 405512 | tf_op jit(solution)/shard_map/ppermute | solution.py:507
  148.6 6.5 %collective-permute-start.29 = (bf16[528,128]{1,0:T(8,128)(2,1)S(1)}, bf16[528,128]{1,0:T(8,128)(2,1)S(1)}, u32[]{:S(2)}, u32[]{:S(2)}) collective-permute-start(bf16[528,128]{1,0:T(8,128)(2,1)S(1)} %get-tuple-element.81), channel_id=1, source_target_pairs={{0,1},{1,0},{2,3},{3,2},{4,5},{5,4},{6,7},{7,6},{8,9},{9,8},{10,11... | collective-permute-start | bytes 405512 | tf_op jit(solution)/shard_map/ppermute | solution.py:507
  151.5 7.2 %collective-permute-start.39 = (bf16[528,128]{1,0:T(8,128)(2,1)S(1)}, bf16[528,128]{1,0:T(8,128)(2,1)S(1)}, u32[]{:S(2)}, u32[]{:S(2)}) collective-permute-start(bf16[528,128]{1,0:T(8,128)(2,1)S(1)} %get-tuple-element.92), channel_id=1, source_target_pairs={{0,12},{1,13},{2,14},{3,15},{4,8},{5,9},{6,10},{7,11},{8,4},{9,5},... | collective-permute-start | bytes 405512 | tf_op jit(solution)/shard_map/ppermute | solution.py:507
  154.0 11.3 %collective-permute-start.40 = (bf16[528,128]{1,0:T(8,128)(2,1)S(1)}, bf16[528,128]{1,0:T(8,128)(2,1)S(1)}, u32[]{:S(2)}, u32[]{:S(2)}) collective-permute-start(bf16[528,128]{1,0:T(8,128)(2,1)S(1)} %get-tuple-element.93), channel_id=1, source_target_pairs={{0,8},{1,9},{2,10},{3,11},{4,12},{5,13},{6,14},{7,15},{8,0},{9,1},... | collective-permute-start | bytes 405512 | tf_op jit(solution)/shard_map/ppermute | solution.py:507
  154.0 11.3 %collective-permute-start.41 = (bf16[528,128]{1,0:T(8,128)(2,1)S(1)}, bf16[528,128]{1,0:T(8,128)(2,1)S(1)}, u32[]{:S(2)}, u32[]{:S(2)}) collective-permute-start(bf16[528,128]{1,0:T(8,128)(2,1)S(1)} %get-tuple-element.94), channel_id=1, source_target_pairs={{0,4},{1,5},{2,6},{3,7},{4,0},{5,1},{6,2},{7,3},{8,12},{9,13},{10,... | collective-permute-start | bytes 405512 | tf_op jit(solution)/shard_map/ppermute | solution.py:507
